TPU v7x, 128 devices: a whole 4x4x4 slice. The times are simulated.
128 devices in a mesh: lon: 16 (over y_hi, z, core), lat: 8 (over x, y_lo).
Axes of the slice: x: 4, y: 4 (y_hi: 2, y_lo: 2; y = y_hi * 2 + y_lo), z: 4, core: 2. Of those that a mesh axis runs over, the one named last changes fastest.
Arguments:
- tracers: float32 [4, 1024, 512, 128], P(None, 'lon', 'lat'), may hold values from 0.2 to 2
- kdiff: float32 [1024, 512, 128], P('lon', 'lat'), may hold values from 0.3 to 8
- photolysis: float32 [1024, 512, 128], P('lon', 'lat'), may hold values from 0.05 to 2
- u_wind: float32 [1024, 512, 128], P('lon', 'lat'), may hold values from -0.24 to 0.24
- v_wind: float32 [1024, 512, 128], P('lon', 'lat'), may hold values from -0.24 to 0.24
- day_count: int32 [16, 8], replicated, may hold values from 0 to 32, as said below
- day_order: int32 [16, 8, 32], P('lon', 'lat'), may hold values from 0 to 31, each once within a row
Outputs:
- tracers_next: float32 [4, 1024, 512, 128], P(None, 'lon', 'lat')
Inputs may be any that keep to these rules, and one draw needn't show every extreme that they name: Tile (i, j) has day_count[i, j] daylit blocks, named by the first entries of day_order[i, j, :].
All inputs are finite; a program needn't handle non-finite values.
Results may differ from a plain program's by a relative error of at most 0.00002.
Values sent between devices are 32-bit elements; how exact they have to be, the bound alone decides.
A program may use at most 128 MiB of HBM per device.

v0:
```python
import math

import jax
import jax.numpy as jnp
from jax import lax
from jax.sharding import PartitionSpec as P

SECTIONS = 12


def from_behind(value, axis, steps):
    count = lax.axis_size(axis)
    pairs = [(source, (source + steps) % count) for source in range(count)]
    return lax.ppermute(value, axis, pairs)


def with_halo(cells, sides, width, closed):
    for axis, dim in sides:
        count = lax.axis_size(axis)
        ends = count if closed else count - 1
        head = lax.slice_in_dim(cells, 0, width, axis=dim)
        tail = lax.slice_in_dim(cells, cells.shape[dim] - width, cells.shape[dim], axis=dim)
        cells = jnp.concatenate(
            [
                lax.ppermute(tail, axis, [(i, (i + 1) % count) for i in range(ends)]),
                cells,
                lax.ppermute(head, axis, [((i + 1) % count, i) for i in range(ends)]),
            ],
            axis=dim,
        )
    return cells


def section_table(sections):
    bvals = [1.0 / 3.0] * 3 + [
        (j * j + j - 2.0) / (2.0 * j * (j + 1.0)) for j in range(3, sections + 1)
    ]
    scale = 4.0 / (sections * sections + sections - 2.0)
    rows = []
    for j in range(2, sections + 1):
        coef_prev = (2.0 * j - 1.0) / j * bvals[j] / bvals[j - 1]
        coef_back = -(j - 1.0) / j * bvals[j] / bvals[j - 2]
        coef_step = coef_prev * scale
        coef_first = -(1.0 - bvals[j - 1]) * coef_step
        rows.append((coef_prev, coef_back, 1.0 - coef_prev - coef_back, coef_step, coef_first))
    return (bvals[1] * scale, rows)


def tendency(field, diffusion, photo):
    above = jnp.concatenate([field[..., 1:], field[..., -1:]], axis=-1)
    upward = diffusion * (above - field)
    below = jnp.concatenate([jnp.zeros_like(upward[..., :1]), upward[..., :-1]], axis=-1)
    mixing = upward - below
    ozone, oxygen, nitric, dioxide = (field[0], field[1], field[2], field[3])
    titration = ozone * nitric
    split_no2 = 2.0 * photo * dioxide
    split_o3 = 0.25 * photo * ozone
    chemistry = jnp.stack(
        [
            1.5 * oxygen - titration - split_o3,
            split_no2 + split_o3 - 1.5 * oxygen,
            split_no2 - titration,
            titration - split_no2,
        ],
        axis=0,
    )
    return mixing + 0.5 * chemistry


def column_step(field, diffusion, photo):
    first_coef, table = section_table(SECTIONS)
    start_rate = tendency(field, diffusion, photo)
    previous = field
    current = field + first_coef * start_rate
    for coef_prev, coef_back, coef_base, coef_step, coef_first in table:
        following = (
            coef_prev * current
            + coef_back * previous
            + coef_base * field
            + coef_step * tendency(current, diffusion, photo)
            + coef_first * start_rate
        )
        previous, current = (current, following)
    return current


def night_step(field):
    ozone, oxygen, nitric = (field[0], field[1], field[2])
    titration = ozone * nitric
    change = jnp.stack([1.5 * oxygen - titration, -1.5 * oxygen, -titration, titration], axis=0)
    return field + 0.5 * change


def pick_blocks(blocks, diff_blocks, photo_blocks, block_ids):
    return jnp.concatenate(
        [
            jnp.take(blocks, block_ids, axis=1),
            jnp.take(diff_blocks, block_ids, axis=0)[None],
            jnp.take(photo_blocks, block_ids, axis=0)[None],
        ],
        axis=0,
    )


def advance_parcel(parcel, species):
    return column_step(parcel[:species], parcel[species], parcel[species + 1])


def local_pass(totals, blocks, diff_blocks, photo_blocks, ordering, slot_count, group_slots):
    species = blocks.shape[0]
    block_count = ordering.shape[0]
    turns = (slot_count + group_slots - 1) // group_slots

    def one_turn(turn, running):
        slots = turn * group_slots + jnp.arange(group_slots, dtype=jnp.int32)
        valid = slots < slot_count
        block_ids = ordering[jnp.clip(slots, 0, block_count - 1)]
        parcel = pick_blocks(blocks, diff_blocks, photo_blocks, block_ids)
        advanced = advance_parcel(parcel, species)
        targets = jnp.where(valid, block_ids, block_count)
        return running.at[:, targets].set(advanced, mode="drop")

    return lax.fori_loop(jnp.int32(0), turns, one_turn, totals)


def body(tracers, kdiff, photolysis, u_wind, v_wind, day_count, day_order):
    species, lon_cells, lat_cells, levels = tracers.shape
    ordering = day_order[0, 0]
    block_count = ordering.shape[0]
    block_cols = lon_cells * lat_cells // block_count
    half_slots = block_count // 2
    group_slots = math.gcd(4, half_slots)
    lon_devices = lax.axis_size("lon")
    half_turn = lon_devices // 2
    lon_place = lax.axis_index("lon")
    lat_place = lax.axis_index("lat")
    own_count = day_count[lon_place, lat_place]
    mate_count = day_count[(lon_place + half_turn) % lon_devices, lat_place]
    blocks = tracers.reshape(species, block_count, block_cols, levels)
    diff_blocks = kdiff.reshape(block_count, block_cols, levels)
    photo_blocks = photolysis.reshape(block_count, block_cols, levels)
    stepped = night_step(blocks)
    send_count = jnp.maximum(own_count - mate_count, 0) // 2
    recv_count = jnp.maximum(mate_count - own_count, 0) // 2
    offsets = jnp.arange(half_slots, dtype=jnp.int32)
    slots = own_count - send_count + offsets
    valid = offsets < send_count
    block_ids = ordering[jnp.clip(slots, 0, block_count - 1)]
    parcel = pick_blocks(blocks, diff_blocks, photo_blocks, block_ids)
    arrived = from_behind(parcel, "lon", half_turn)
    stepped = local_pass(
        stepped, blocks, diff_blocks, photo_blocks, ordering, own_count - send_count, group_slots
    )
    results = jnp.zeros((species, half_slots, block_cols, levels), jnp.float32)
    turns = (recv_count + group_slots - 1) // group_slots

    def remote_turn(turn, running):
        portion = lax.dynamic_slice_in_dim(arrived, turn * group_slots, group_slots, 1)
        advanced = advance_parcel(portion, species)
        return lax.dynamic_update_slice_in_dim(running, advanced, turn * group_slots, 1)

    results = lax.fori_loop(jnp.int32(0), turns, remote_turn, results)
    returned = from_behind(results, "lon", half_turn)
    targets = jnp.where(valid, block_ids, block_count)
    stepped = stepped.at[:, targets].set(returned, mode="drop")
    current = stepped.reshape(species, lon_cells, lat_cells, levels)
    lon_ext = with_halo(jnp.concatenate([current, u_wind[None]], axis=0), (("lon", 1),), 1, True)
    lat_ext = with_halo(jnp.concatenate([current, v_wind[None]], axis=0), (("lat", 2),), 1, False)
    tracer_lon, u_ext = (lon_ext[:species], lon_ext[species])
    tracer_lat, v_ext = (lat_ext[:species], lat_ext[species])
    face_x = (
        jnp.maximum(u_ext[:-1], 0.0) * tracer_lon[:, :-1]
        + jnp.minimum(u_ext[:-1], 0.0) * tracer_lon[:, 1:]
    )
    east = face_x[:, 1:]
    west = face_x[:, :-1]
    face_y = (
        jnp.maximum(v_ext[:, :-1], 0.0) * tracer_lat[:, :, :-1]
        + jnp.minimum(v_ext[:, :-1], 0.0) * tracer_lat[:, :, 1:]
    )
    north = face_y[:, :, 1:]
    south = face_y[:, :, :-1]
    return current - (east - west) - (north - south)


def solution(mesh):
    return jax.shard_map(
        body,
        mesh=mesh,
        in_specs=(
            P(None, "lon", "lat", None),
            P("lon", "lat", None),
            P("lon", "lat", None),
            P("lon", "lat", None),
            P("lon", "lat", None),
            P(),
            P("lon", "lat", None),
        ),
        out_specs=P(None, "lon", "lat", None),
        check_vma=False,
    )
```

profile of v0, /device:TPU:84, one launch (start us, length us, event | category | flops | bytes accessed | tf_op | source)
XLA Modules:
  0.0 656.2 jit_solution(10993075624854990644)
XLA Ops:
  5.3 2.2 gather_fusion.7
  7.5 2.2 gather_fusion.6
  9.7 6.2 gather_fusion.5
  15.9 2.6 select_bitcast_fusion.1
  18.8 3.1 pad_maximum_fusion.8
  23.5 3.7 slice_multiply_fusion.58
  27.8 6.4 fusion.200
  34.2 126.8 %collective-permute-done = f32[6,16,128,128]{3,2,0,1:T(8,128)} collective-permute-done((f32[6,16,128,128]{3,2,0,1:T(8,128)}, f32[6,16,128,128]{3,2,0,1:T(8,128)}, u32[]{:S(2)}, u32[]{:S(2)}) %collective-permute-start) | collective-permute-done | bytes 6291488 | tf_op jit(solution)/shard_map/ppermute | solution.py:14
  161.0 2.6 broadcast_in_dim.66
  163.5 245.0 %while.21 = (s32[]{:T(128)}, f32[4,16,128,128]{3,2,1,0:T(8,128)}, s32[]{:T(128)}, f32[6,16,128,128]{3,2,0,1:T(8,128)}, s32[]{:T(128)}, /*index=5*/s32[]{:T(128)}...) while((s32[]{:T(128)}, f32[4,16,128,128]{3,2,1,0:T(8,128)}, s32[]{:T(128)}, ...), condition=%wide.region_4.7_spmd, body=%wide.region_3.6_spmd.sunk | while | flops 65798156 | bytes 192341408 | solution.py:162
  184.3 2.0 fusion.307
  188.5 2.0 fusion.309
  192.7 2.0 fusion.311
  196.9 2.0 fusion.313
  201.1 2.0 fusion.315
  205.3 2.0 fusion.317
  209.5 2.0 fusion.319
  213.7 2.0 fusion.321
  217.9 3.0 fusion.323
  241.4 2.0 fusion.307
  245.6 2.0 fusion.309
  249.8 2.0 fusion.311
  254.0 2.0 fusion.313
  258.2 2.0 fusion.315
  262.5 2.0 fusion.317
  266.7 2.0 fusion.319
  270.9 2.0 fusion.321
  275.1 3.0 fusion.323
  298.6 2.0 fusion.307
  302.8 2.0 fusion.309
  307.0 2.0 fusion.311
  311.2 2.0 fusion.313
  315.4 2.0 fusion.315
  319.6 2.0 fusion.317
  332.3 3.1 fusion.323
  364.2 2.0 fusion.311
  368.4 2.0 fusion.313
  385.2 2.0 fusion.321
  389.4 3.1 fusion.323
  408.6 5.7 while.20
  414.4 46.3 %collective-permute-done.1 = f32[4,16,128,128]{3,2,1,0:T(8,128)} collective-permute-done((f32[4,16,128,128]{3,2,1,0:T(8,128)}, f32[4,16,128,128]{3,2,1,0:T(8,128)}, u32[]{:S(2)}, u32[]{:S(2)}) %collective-permute-start.1) | collective-permute-done | bytes 4194336 | tf_op jit(solution)/shard_map/ppermute | solution.py:14
  460.7 4.7 copy.163
  465.4 5.6 scatter_fusion.1
  473.0 142.6 %collective-permute-start.5 = (f32[5,64,1,128]{3,1,2,0:T(8,128)S(1)}, f32[5,64,1,128]{3,1,2,0:T(8,128)S(1)}, u32[]{:S(2)}, u32[]{:S(2)}) collective-permute-start(f32[5,64,1,128]{3,1,2,0:T(8,128)S(1)} %bitcast.1129), channel_id=1, source_target_pairs={{1,0},{2,1},{3,2},{4,3},{5,4},{6,5},{7,6},{9,8},{10,9},{11,10},{12... | collective-permute-start | bytes 491528 | tf_op jit(solution)/shard_map/ppermute | solution.py:27
  619.5 4.3 collective-permute-done.4
  624.5 5.9 fusion.193
  630.9 5.3 fusion.196
  636.3 19.6 %fusion.198 = f32[4,64,64,128]{3,2,1,0:T(8,128)} fusion(f32[4,64,65,128]{3,2,1,0:T(8,128)} %fusion.193, f32[4,64,64,128]{3,2,1,0:T(8,128)} %bitcast.1077, f32[4,65,64,128]{3,2,1,0:T(8,128)} %fusion.196), kind=kLoop, calls=%fused_computation.464 | loop fusion | flops 8388608 | bytes 50331648 | tf_op jit(solution)/shard_map/sub | solution.py:183
  (254 shorter events, 175.9 us)
Async XLA Ops:
  21.9 139.1 %collective-permute-start = (f32[6,16,128,128]{3,2,0,1:T(8,128)}, f32[6,16,128,128]{3,2,0,1:T(8,128)}, u32[]{:S(2)}, u32[]{:S(2)}) collective-permute-start(f32[6,16,128,128]{3,2,0,1:T(8,128)} %pad_maximum_fusion.8), channel_id=1, source_target_pairs={{0,64},{8,72},{16,80},{24,88},{32,96},{40,104},{48,112},{56,120},{... | collective-permute-start | bytes 18874376 | tf_op jit(solution)/shard_map/ppermute | solution.py:14
  163.5 245.1 %copy-start = (s32[1,1,32]{2,1,0:T(1,128)S(1)}, s32[1,1,32]{2,1,0:T(1,128)}, u32[]{:S(2)}) copy-start(s32[1,1,32]{2,1,0:T(1,128)} %param.21) | copy-start | bytes 388
  408.5 52.2 %collective-permute-start.1 = (f32[4,16,128,128]{3,2,1,0:T(8,128)}, f32[4,16,128,128]{3,2,1,0:T(8,128)}, u32[]{:S(2)}, u32[]{:S(2)}) collective-permute-start(f32[4,16,128,128]{3,2,1,0:T(8,128)} %get-tuple-element.74), channel_id=1, source_target_pairs={{0,64},{8,72},{16,80},{24,88},{32,96},{40,104},{48,112},{56,120},{... | collective-permute-start | bytes 12582920 | tf_op jit(solution)/shard_map/ppermute | solution.py:14
  414.4 51.0 %copy-start.4 = (s32[16]{0:T(128)S(1)}, s32[16]{0:T(128)}, u32[]{:S(2)}) copy-start(s32[16]{0:T(128)} %get-tuple-element.236) | copy-start | bytes 196
  465.4 5.6 copy-start.2
  471.0 146.6 %copy-start.1 = (f32[4,32,128,128]{3,2,1,0:T(8,128)S(1)}, f32[4,32,128,128]{3,2,1,0:T(8,128)}, u32[]{:S(2)}) copy-start(f32[4,32,128,128]{3,2,1,0:T(8,128)} %scatter_fusion.1) | copy-start | bytes 25165828
  471.0 146.6 %copy-start.3 = (f32[64,64,128]{2,1,0:T(8,128)S(1)}, f32[64,64,128]{2,1,0:T(8,128)}, u32[]{:S(2)}) copy-start(f32[64,64,128]{2,1,0:T(8,128)} %param.18) | copy-start | bytes 6291460
  473.0 146.4 %collective-permute-start.5 = (f32[5,64,1,128]{3,1,2,0:T(8,128)S(1)}, f32[5,64,1,128]{3,1,2,0:T(8,128)S(1)}, u32[]{:S(2)}, u32[]{:S(2)}) collective-permute-start(f32[5,64,1,128]{3,1,2,0:T(8,128)S(1)} %bitcast.1129), channel_id=1, source_target_pairs={{1,0},{2,1},{3,2},{4,3},{5,4},{6,5},{7,6},{9,8},{10,9},{11,10},{12... | collective-permute-start | bytes 491528 | tf_op jit(solution)/shard_map/ppermute | solution.py:27
  615.7 8.1 %collective-permute-start.4 = (f32[5,64,1,128]{3,1,2,0:T(8,128)S(1)}, f32[5,64,1,128]{3,1,2,0:T(8,128)S(1)}, u32[]{:S(2)}, u32[]{:S(2)}) collective-permute-start(f32[5,64,1,128]{3,1,2,0:T(8,128)S(1)} %bitcast.1128), channel_id=1, source_target_pairs={{0,1},{1,2},{2,3},{3,4},{4,5},{5,6},{6,7},{8,9},{9,10},{10,11},{11... | collective-permute-start | bytes 491528 | tf_op jit(solution)/shard_map/ppermute | solution.py:25
  617.6 12.7 %collective-permute-start.2 = (f32[5,1,64,128]{3,2,1,0:T(8,128)S(1)}, f32[5,1,64,128]{3,2,1,0:T(8,128)S(1)}, u32[]{:S(2)}, u32[]{:S(2)}) collective-permute-start(f32[5,1,64,128]{3,2,1,0:T(8,128)S(1)} %get-tuple-element.222), channel_id=1, source_target_pairs={{0,8},{8,16},{16,24},{24,32},{32,40},{40,48},{48,56},{56,64},{64,7... | collective-permute-start | bytes 491528 | tf_op jit(solution)/shard_map/ppermute | solution.py:25
  617.7 13.2 %collective-permute-start.3 = (f32[5,1,64,128]{3,2,1,0:T(8,128)S(1)}, f32[5,1,64,128]{3,2,1,0:T(8,128)S(1)}, u32[]{:S(2)}, u32[]{:S(2)}) collective-permute-start(f32[5,1,64,128]{3,2,1,0:T(8,128)S(1)} %get-tuple-element.223), channel_id=1, source_target_pairs={{8,0},{16,8},{24,16},{32,24},{40,32},{48,40},{56,48},{64,56},{72,6... | collective-permute-start | bytes 491528 | tf_op jit(solution)/shard_map/ppermute | solution.py:27
where the time goes:
time: 666 us; the launch traced here: 656 us
  other arithmetic  234 us (35%)
  waiting for transfers between devices  177 us (27%)
  starting transfers between devices  147 us (22%)
  local copies, waits for them, and re-layouts  71.3 us (11%)
  loops' own time  23 us (3%)
    ppermute x2, waiting for transfers between devices, from_behind(): return lax.ppermute(value, axis, pairs)  173 us
    ppermute x2, starting transfers between devices, with_halo(): lax.ppermute(head, axis, [((i + 1) % count, i) for i in range(ends)])  144 us
    add x40, other arithmetic, column_step(): coef_prev * current + coef_back * previous + coef_base * field  81 us
    sub x44, other arithmetic, tendency(): 1.5 * oxygen - titration - split_o3  48.1 us
    slice x92, local copies, waits for them, and re-layouts, tendency(): above = jnp.concatenate([field[..., 1:], field[..., -1:]], axis=-1)  36 us
    mul x48, other arithmetic, tendency(): upward = diffusion * (above - field)  29.1 us
    sub x1, other arithmetic, body(): return current - (east - west) - (north - south)  19.6 us
    another operation x1, loops' own time, body(): results = lax.fori_loop(jnp.int32(0), turns, remote_turn, results)  17.3 us
  transfers between devices with their start and end apart: 6, of which 3 were waited for; matrix products, arithmetic and copies ran while one was open for 3% of the time, Pallas kernels for 0%

commit v1 on v0

v1 whole, which is shorter than its diff:
```python
import functools

import jax
import jax.numpy as jnp
from jax import lax
from jax.experimental import pallas as pl
from jax.experimental.pallas import tpu as pltpu
from jax.sharding import PartitionSpec as P

SECTIONS = 12
LEV = 128
UNROLL = 32
F32 = jnp.float32
ANY = pl.BlockSpec(memory_space=pl.ANY)
SMEM = pl.BlockSpec(memory_space=pltpu.SMEM)


def section_table(sections):
    bvals = [1.0 / 3.0] * 3 + [
        (j * j + j - 2.0) / (2.0 * j * (j + 1.0)) for j in range(3, sections + 1)
    ]
    scale = 4.0 / (sections * sections + sections - 2.0)
    lead = [1.0, 1.0]
    for j in range(2, sections + 1):
        lead.append(lead[-1] * (2.0 * j - 1.0) / j)
    return bvals, scale, lead


BVALS, SCALE, LEAD = section_table(SECTIONS)


def level_rows(level):
    return pl.ds(pl.multiple_of(level * 8, 8), 8)


def stage(j, cur, old, out, first, kdt, pht, tit):
    keep, share, lead = 1.0 - BVALS[j - 1], BVALS[j - 1], LEAD[j - 1]
    shift = keep / (share * lead)
    product = SCALE * share * lead / 2.0
    offset = SCALE * shift / 2.0
    decay = 0.75 * SCALE
    back = (j - 1.0) / j * LEAD[j - 2] / LEAD[j] if j > 1 else 0.0

    def step(i, carry):
        here, below = list(carry[:4]), list(carry[4:])
        for r in range(UNROLL):
            level = i * UNROLL + r
            rows, above_rows = level_rows(level), level_rows(level + 1)
            mixing = kdt[rows, :]
            above = [cur[q, above_rows, :] for q in range(4)]
            upward = [mixing * (above[q] - here[q]) for q in range(4)]
            state = [(here[q] + upward[q]) - below[q] for q in range(4)]
            if j == 1:
                titration = (SCALE / 2.0) * tit[rows, :]
            else:
                titration = (
                    product
                    * (here[0] + shift * first[0, rows, :])
                    * (here[2] + shift * first[2, rows, :])
                    - offset * tit[rows, :]
                )
            split = pht[0, rows, :] * here[3]
            net = split - titration
            joined = decay * here[1] - pht[1, rows, :] * here[0]
            state = [
                state[0] + (joined - titration),
                state[1] + (split - joined),
                state[2] + net,
                state[3] - net,
            ]
            if j > 1:
                state = [state[q] - back * old[q, rows, :] for q in range(4)]
            for q in range(4):
                out[q, rows, :] = state[q]
            here, below = above, upward
        return (*here, *below)

    zero = jnp.zeros((8, LEV), F32)
    init = tuple(cur[q, pl.ds(0, 8), :] for q in range(4)) + (zero,) * 4
    lax.fori_loop(0, LEV // UNROLL, step, init)


def advance_group(y_nat, k_nat, p_nat, row0, work, ready, lit_of, put):
    first, ping, pong, kdt, pht, tit = work
    zero = jnp.zeros((8, LEV), F32)

    def tile_in(tile, carry):
        src = pl.ds(pl.multiple_of(row0 + tile * 128, 8), 128)
        dst = pl.ds(tile, 128, stride=8)
        for q in range(4):
            first[q, dst, :] = y_nat[q, src, :].T
        kdt[dst, :] = (SCALE * k_nat[src, :]).T
        light = (SCALE * p_nat[src, :]).T
        pht[0, dst, :] = light
        pht[1, dst, :] = 0.125 * light
        return carry

    tile = 0
    for count, wait in ready:
        wait()
        lax.fori_loop(tile, tile + count, tile_in, 0)
        tile += count
    kdt[pl.ds(LEV * 8 - 8, 8), :] = zero
    for q in range(4):
        for ref in (first, ping, pong):
            ref[q, pl.ds(LEV * 8, 8), :] = zero

    def products(i, carry):
        for r in range(16):
            rows = level_rows(i * 16 + r)
            tit[rows, :] = first[0, rows, :] * first[2, rows, :]
        return carry

    lax.fori_loop(0, LEV // 16, products, 0)
    cur, old = first, None
    for j in range(1, SECTIONS + 1):
        out = ping if j % 2 else pong
        stage(j, cur, old, out, first, kdt, pht, tit)
        cur, old = out, cur
    keep = 1.0 - BVALS[SECTIONS]
    share = BVALS[SECTIONS] * LEAD[SECTIONS]

    def tile_out(tile, carry):
        dst = pl.ds(tile, 128, stride=8)
        day = [(keep * first[q, dst, :] + share * cur[q, dst, :]).T for q in range(4)]
        for r in range(16):
            octet = tile * 16 + r
            rows = pl.ds(pl.multiple_of(row0 + octet * 8, 8), 8)
            ozone, oxygen, nitric, dioxide = [y_nat[q, rows, :] for q in range(4)]
            half = 0.5 * (ozone * nitric)
            gain = 0.75 * oxygen
            night = [ozone + (gain - half), oxygen - gain, nitric - half, dioxide + half]
            lit = jnp.full((8, LEV), lit_of(octet), jnp.int32) > 0
            put(octet, rows, [jnp.where(lit, day[q][r * 8 : r * 8 + 8], night[q]) for q in range(4)])
        return carry

    lax.fori_loop(0, 8, tile_out, 0)


def fill_lit(lit, count_ref, order_ref):
    count = count_ref[lax.axis_index("lon"), lax.axis_index("lat")]

    def mark(i, carry):
        lit[order_ref[0, 0, i]] = (i < count).astype(jnp.int32)
        return carry

    lax.fori_loop(0, lit.shape[0], mark, 0)


def sixth(n):
    return lax.shift_right_logical(n * 10923, 16)


def inner_longitude(octet):
    place = sixth(octet)
    return jnp.where(place == 0, 0, jnp.where(place == 1, 63, place - 1))


class Copies:
    def __init__(self, sems):
        self.sems, self.used = sems, 0

    def start(self, pairs):
        group = []
        for src, dst in pairs:
            copy = pltpu.make_async_copy(src, dst, self.sems.at[self.used])
            self.used += 1
            copy.start()
            group.append(copy)
        return lambda: [copy.wait() for copy in group]


def flat(ref):
    return ref.reshape(*ref.shape[:-3], ref.shape[-3] * ref.shape[-2], LEV)


def edge_kernel(
    y, k, p, u, v, count, order,
    polar, inner, north_row, south_row, east_row, west_row,
    ty1, tk1, tp1, ty2, tk2, tp2, urow, vrow, lit, *rest,
):
    work, sems = rest[:-1], rest[-1]
    copies = Copies(sems)
    ready = []
    for c in range(4):
        lons = pl.ds(16 * c, 16)
        pairs = []
        for lats, rows in ((pl.ds(0, 8), pl.ds(0, 8)), (pl.ds(56, 8), pl.ds(8, 8))):
            pairs.append((y.at[:, lons, lats], ty1.at[:, lons, rows]))
            pairs.append((k.at[lons, lats], tk1.at[lons, rows]))
            pairs.append((p.at[lons, lats], tp1.at[lons, rows]))
        ready.append((2, copies.start(pairs)))
    lats = pl.ds(8, 48)
    pairs = [(u.at[63], urow), (v.at[:, 63], vrow)]
    for src, dst in ((pl.ds(0, 1), pl.ds(0, 1)), (pl.ds(63, 1), pl.ds(1, 1)), (pl.ds(1, 20), pl.ds(2, 20))):
        pairs.append((y.at[:, src, lats], ty2.at[:, dst]))
        pairs.append((k.at[src, lats], tk2.at[dst]))
        pairs.append((p.at[src, lats], tp2.at[dst]))
    second = copies.start(pairs)
    fill_lit(lit, count, order)

    y1, y2 = flat(ty1), flat(ty2)

    def put1(octet, rows, values):
        for q in range(4):
            y1[q, rows, :] = values[q]

    def put2(octet, rows, values):
        for q in range(4):
            y2[q, rows, :] = values[q]

    advance_group(
        y1, flat(tk1), flat(tp1), 0, work, ready,
        lambda octet: lit[lax.shift_right_logical(octet, 2)], put1,
    )
    second()
    done1 = copies.start([
        (urow, west_row.at[4]),
        (vrow, south_row.at[4]),
        (ty1, polar),
        (ty1.at[:, :, 0], north_row),
        (ty1.at[:, :, 15], south_row.at[pl.ds(0, 4)]),
        (ty1.at[:, 0, pl.ds(0, 8)], east_row.at[:, pl.ds(0, 8)]),
        (ty1.at[:, 0, pl.ds(8, 8)], east_row.at[:, pl.ds(56, 8)]),
        (ty1.at[:, 63, pl.ds(0, 8)], west_row.at[pl.ds(0, 4), pl.ds(0, 8)]),
        (ty1.at[:, 63, pl.ds(8, 8)], west_row.at[pl.ds(0, 4), pl.ds(56, 8)]),
    ])
    advance_group(
        y2, flat(tk2), flat(tp2), 0, work, [(8, lambda: None)],
        lambda octet: lit[lax.shift_right_logical(inner_longitude(octet), 1)], put2,
    )
    done2 = copies.start([
        (ty2, inner),
        (ty2.at[:, 0], east_row.at[:, pl.ds(8, 48)]),
        (ty2.at[:, 1], west_row.at[pl.ds(0, 4), pl.ds(8, 48)]),
    ])
    done1()
    done2()


def load_inner(copies, y, k, p, ty, tk, tp, lon0):
    lats = pl.ds(8, 48)
    ready = []
    for c in range(2):
        src, dst = pl.ds(lon0 + 11 * c, 11), pl.ds(11 * c, 11)
        ready.append((4, copies.start([
            (y.at[:, src, lats], ty.at[:, dst]),
            (k.at[src, lats], tk.at[dst]),
            (p.at[src, lats], tp.at[dst]),
        ])))
    return ready


def middle_kernel(y, k, p, count, order, inner, ty, tk, tp, lit, *rest):
    work, sems = rest[:-1], rest[-1]
    copies = Copies(sems)
    ready = load_inner(copies, y, k, p, ty, tk, tp, 20)
    fill_lit(lit, count, order)
    flat_y = flat(ty)

    def put(octet, rows, values):
        for q in range(4):
            flat_y[q, rows, :] = values[q]

    advance_group(
        flat_y, flat(tk), flat(tp), 16, work, ready,
        lambda octet: lit[lax.shift_right_logical(inner_longitude(octet + 128), 1)], put,
    )
    copies.start([(ty, inner)])()


CHUNK = 4


def last_kernel(
    y, k, p, u, v, count, order, polar, inner1, inner2, own_row, h_north, h_south, h_east, h_west,
    out,
    ty, tk, tp, mixed, uwind, vwind, first_row, s_halo, w_halo, south, eastward, northward, stage_out, lit,
    *rest,
):
    work, out_sems, sems = rest[:-2], rest[-2], rest[-1]
    copies = Copies(sems)
    ready = load_inner(copies, y, k, p, ty, tk, tp, 41)
    fill_lit(lit, count, order)
    body = pl.ds(1, 64)
    lats = pl.ds(16, 48)
    filled = copies.start([
        (u, uwind),
        (v, vwind),
        (own_row, first_row),
        (h_south, s_halo),
        (h_west, w_halo),
        (h_north, mixed.at[:, body, 72]),
        (h_east, mixed.at[:, 65, pl.ds(8, 64)]),
        (polar.at[:, :, pl.ds(0, 8)], mixed.at[:, body, pl.ds(8, 8)]),
        (polar.at[:, :, pl.ds(8, 8)], mixed.at[:, body, pl.ds(64, 8)]),
        (inner1.at[:, 0], mixed.at[:, 1, lats]),
        (inner1.at[:, 1], mixed.at[:, 64, lats]),
        (inner1.at[:, pl.ds(2, 19)], mixed.at[:, pl.ds(2, 19), lats]),
        (inner1.at[:, 21, pl.ds(0, 16)], mixed.at[:, 21, pl.ds(16, 16)]),
        (inner2.at[:, 0, pl.ds(16, 32)], mixed.at[:, 21, pl.ds(32, 32)]),
        (inner2.at[:, pl.ds(1, 20)], mixed.at[:, pl.ds(22, 20), lats]),
        (inner2.at[:, 21, pl.ds(0, 32)], mixed.at[:, 42, pl.ds(16, 32)]),
    ])

    def put(octet, rows, values):
        place = sixth(octet + 256)
        part = octet + 256 - 6 * place
        dst = pl.ds(pl.multiple_of(part * 8 + 16, 8), 8)
        for q in range(4):
            mixed[q, place, dst, :] = values[q]

    advance_group(
        flat(ty), flat(tk), flat(tp), 32, work, ready,
        lambda octet: lit[lax.shift_right_logical(sixth(octet + 256) - 1, 1)], put,
    )
    filled()
    for m in range(8):
        rows = pl.ds(8 * m, 8)
        wind, gust = w_halo[4, rows, :], s_halo[4, rows, :]
        for q in range(4):
            eastward[q, rows, :] = wind * jnp.where(
                wind > 0, w_halo[q, rows, :], mixed[q, 1, pl.ds(8 + 8 * m, 8), :]
            )
            south[q, rows, :] = gust * jnp.where(gust > 0, s_halo[q, rows, :], first_row[q, rows, :])

    def out_copy(chunk, slot):
        return pltpu.make_async_copy(
            stage_out.at[slot], out.at[:, pl.ds(chunk * CHUNK, CHUNK)], out_sems.at[slot]
        )

    def chunk_step(chunk, carry):
        slot = lax.rem(chunk, 2)

        @pl.when(chunk >= 2)
        def _():
            out_copy(chunk - 2, slot).wait()

        def lon_step(local, inner_carry):
            lon = chunk * CHUNK + local
            for q in range(4):
                northward[q, pl.ds(7, 1), :] = south[q, pl.ds(lon, 1), :]
            for m in range(8):
                rows = pl.ds(8 * m, 8)
                here_rows = pl.ds(8 + 8 * m, 8)
                wind, gust = uwind[lon, rows, :], vwind[lon, rows, :]
                wind_up, gust_up = wind > 0, gust > 0
                for q in range(4):
                    here = mixed[q, lon + 1, here_rows, :]
                    east = wind * jnp.where(wind_up, here, mixed[q, lon + 2, here_rows, :])
                    north = gust * jnp.where(gust_up, here, mixed[q, lon + 1, pl.ds(9 + 8 * m, 8), :])
                    west = eastward[q, rows, :]
                    eastward[q, rows, :] = east
                    northward[q, here_rows, :] = north
                    below = northward[q, pl.ds(7 + 8 * m, 8), :]
                    stage_out[slot, q, local, rows, :] = here - (east - west) - (north - below)
            return inner_carry

        lax.fori_loop(0, CHUNK, lon_step, 0)
        out_copy(chunk, slot).start()
        return carry

    chunks = 64 // CHUNK
    lax.fori_loop(0, chunks, chunk_step, 0)
    for chunk in (chunks - 2, chunks - 1):
        out_copy(chunk, chunk % 2).wait()


WORK = [
    pltpu.VMEM((4, LEV * 8 + 8, LEV), F32),
    pltpu.VMEM((4, LEV * 8 + 8, LEV), F32),
    pltpu.VMEM((4, LEV * 8 + 8, LEV), F32),
    pltpu.VMEM((LEV * 8, LEV), F32),
    pltpu.VMEM((2, LEV * 8, LEV), F32),
    pltpu.VMEM((LEV * 8, LEV), F32),
]
INNER = [
    pltpu.VMEM((4, 22, 48, LEV), F32),
    pltpu.VMEM((22, 48, LEV), F32),
    pltpu.VMEM((22, 48, LEV), F32),
]
LIT = pltpu.SMEM((32,), jnp.int32)


def shape(*dims):
    return jax.ShapeDtypeStruct(dims, F32)


def cost(groups):
    return pl.CostEstimate(
        flops=groups * 128 * 1024 * 540, bytes_accessed=groups * 5 * 2**20, transcendentals=0
    )


PARAMS = pltpu.CompilerParams(vmem_limit_bytes=60 * 2**20)


def body(tracers, kdiff, photolysis, u_wind, v_wind, day_count, day_order):
    polar, inner1, north_row, south_row, east_row, west_row = pl.pallas_call(
        edge_kernel,
        name="edge_groups",
        out_shape=(
            shape(4, 64, 16, LEV), shape(4, 22, 48, LEV),
            shape(4, 64, LEV), shape(5, 64, LEV), shape(4, 64, LEV), shape(5, 64, LEV),
        ),
        in_specs=[ANY] * 5 + [SMEM] * 2,
        out_specs=(ANY,) * 6,
        scratch_shapes=[
            pltpu.VMEM((4, 64, 16, LEV), F32),
            pltpu.VMEM((64, 16, LEV), F32),
            pltpu.VMEM((64, 16, LEV), F32),
            *INNER,
            pltpu.VMEM((64, LEV), F32),
            pltpu.VMEM((64, LEV), F32),
            LIT, *WORK, pltpu.SemaphoreType.DMA((48,)),
        ],
        compiler_params=PARAMS,
        cost_estimate=cost(2),
    )(tracers, kdiff, photolysis, u_wind, v_wind, day_count, day_order)

    lats, lons = lax.axis_size("lat"), lax.axis_size("lon")
    h_north = lax.ppermute(north_row, "lat", [(i + 1, i) for i in range(lats - 1)])
    h_south = lax.ppermute(south_row, "lat", [(i, i + 1) for i in range(lats - 1)])
    h_east = lax.ppermute(east_row, "lon", [((i + 1) % lons, i) for i in range(lons)])
    h_west = lax.ppermute(west_row, "lon", [(i, (i + 1) % lons) for i in range(lons)])

    inner2 = pl.pallas_call(
        middle_kernel,
        name="middle_group",
        out_shape=shape(4, 22, 48, LEV),
        in_specs=[ANY] * 3 + [SMEM] * 2,
        out_specs=ANY,
        scratch_shapes=[*INNER, LIT, *WORK, pltpu.SemaphoreType.DMA((8,))],
        compiler_params=PARAMS,
        cost_estimate=cost(1),
    )(tracers, kdiff, photolysis, day_count, day_order)

    return pl.pallas_call(
        last_kernel,
        name="last_group",
        out_shape=shape(4, 64, 64, LEV),
        in_specs=[ANY] * 5 + [SMEM] * 2 + [ANY] * 8,
        out_specs=ANY,
        scratch_shapes=[
            *INNER,
            pltpu.VMEM((4, 66, 80, LEV), F32),
            pltpu.VMEM((64, 64, LEV), F32),
            pltpu.VMEM((64, 64, LEV), F32),
            pltpu.VMEM((4, 64, LEV), F32),
            pltpu.VMEM((5, 64, LEV), F32),
            pltpu.VMEM((5, 64, LEV), F32),
            pltpu.VMEM((4, 64, LEV), F32),
            pltpu.VMEM((4, 64, LEV), F32),
            pltpu.VMEM((4, 72, LEV), F32),
            pltpu.VMEM((2, 4, CHUNK, 64, LEV), F32),
            LIT, *WORK, pltpu.SemaphoreType.DMA((2,)), pltpu.SemaphoreType.DMA((24,)),
        ],
        compiler_params=PARAMS,
        cost_estimate=cost(1),
    )(
        tracers, kdiff, photolysis, u_wind, v_wind, day_count, day_order,
        polar, inner1, inner2, north_row, h_north, h_south, h_east, h_west,
    )


def solution(mesh):
    return jax.shard_map(
        body,
        mesh=mesh,
        in_specs=(
            P(None, "lon", "lat", None),
            P("lon", "lat", None),
            P("lon", "lat", None),
            P("lon", "lat", None),
            P("lon", "lat", None),
            P(),
            P("lon", "lat", None),
        ),
        out_specs=P(None, "lon", "lat", None),
        check_vma=False,
    )
```

time: 666 us -> 82 us (0.12)
  the two profiles are of different devices: /device:TPU:84 before, /device:TPU:2 now
where the time goes in v1:
time: 82 us; the launch traced here: 81.6 us
  Pallas kernels  66.9 us (82%)
  starting transfers between devices  12.3 us (15%)
  local copies, waits for them, and re-layouts  2.13 us (3%)
    pallas_call x1, Pallas kernels, body(): pl.pallas_call(edge_kernel, name='edge_groups', out_shape=(shape(4, 64, 1...  28 us
    pallas_call x1, Pallas kernels, body(): pl.pallas_call(last_kernel, name='last_group', out_shape=shape(4, 64, 64,...  23.3 us
    pallas_call x1, Pallas kernels, body(): pl.pallas_call(middle_kernel, name='middle_group', out_shape=shape(4, 22,...  15.6 us
    ppermute x1, starting transfers between devices, body(): lax.ppermute(east_row, 'lon', [((i + 1) % lons, i) for i in range(lons)])  5.6 us
    ppermute x1, starting transfers between devices, body(): lax.ppermute(south_row, 'lat', [(i, i + 1) for i in range(lats - 1)])  3.48 us
    ppermute x1, starting transfers between devices, body(): lax.ppermute(north_row, 'lat', [(i + 1, i) for i in range(lats - 1)])  3.17 us
    unnamed x9, local copies, waits for them, and re-layouts  2.13 us
  transfers between devices with their start and end apart: 4, of which 0 were waited for; matrix products, arithmetic and copies ran while one was open for 0% of the time, Pallas kernels for 19%

profile of v1, /device:TPU:2, one launch (start us, length us, event | category | flops | bytes accessed | tf_op | source)
XLA Modules:
  0.0 81.6 jit_solution(13412886306198871552)
XLA Ops:
  0.0 1.3 %copy.10.count = s32[16,8]{1,0:T(8,128)} copy(s32[16,8]{0,1:T(8,128)} %param.12) | data formatting | bytes 1024 | tf_op args[5]
  1.3 28.0 %edge_groups.1 = (f32[4,64,16,128]{3,2,1,0:T(8,128)}, f32[4,22,48,128]{3,2,1,0:T(8,128)}, f32[4,64,128]{2,1,0:T(8,128)}, f32[5,64,128]{2,1,0:T(8,128)}, f32[4,64,128]{2,1,0:T(8,128)}, /*index=5*/f32[5,64,128]{2,1,0:T(8,128)}) custom-call(f32[4,64,64,128]{3,2,1,0:T(8,128)} %y.5, f32[64,64,128]{2,1,0:T(8,128)} %k.5, f32[64,64,128]{2,1,0:T(8,128)} %p.5, ...), custom_call_target="tpu_custom_call" | custom-call | flops 141557760 | bytes 10485760 | tf_op jit(solution)/shard_map/edge_groups/pallas_call | solution.py:399
  29.3 3.5 %collective-permute-start.1 = (f32[5,64,128]{2,1,0:T(8,128)}, f32[5,64,128]{2,1,0:T(8,128)S(1)}, u32[]{:S(2)}, u32[]{:S(2)}) collective-permute-start(f32[5,64,128]{2,1,0:T(8,128)} %get-tuple-element.14), channel_id=1, source_target_pairs={{0,1},{1,2},{2,3},{3,4},{4,5},{5,6},{6,7},{8,9},{9,10},{10,11},{11... | collective-permute-start | bytes 491528 | tf_op jit(solution)/shard_map/ppermute | solution.py:423
  32.8 0.1 collective-permute-start.3
  32.9 5.6 %collective-permute-start.2 = (f32[4,64,128]{2,1,0:T(8,128)}, f32[4,64,128]{2,1,0:T(8,128)S(1)}, u32[]{:S(2)}, u32[]{:S(2)}) collective-permute-start(f32[4,64,128]{2,1,0:T(8,128)} %get-tuple-element.15), channel_id=1, source_target_pairs={{8,0},{16,8},{24,16},{32,24},{40,32},{48,40},{56,48},{64,56},{72,6... | collective-permute-start | bytes 393224 | tf_op jit(solution)/shard_map/ppermute | solution.py:424
  38.5 3.2 %collective-permute-start = (f32[4,64,128]{2,1,0:T(8,128)}, f32[4,64,128]{2,1,0:T(8,128)S(1)}, u32[]{:S(2)}, u32[]{:S(2)}) collective-permute-start(f32[4,64,128]{2,1,0:T(8,128)} %get-tuple-element.13.own_row), channel_id=1, source_target_pairs={{1,0},{2,1},{3,2},{4,3},{5,4},{6,5},{7,6},{9,8},{10,9},{11,10},{12... | collective-permute-start | bytes 393224 | tf_op jit(solution)/shard_map/ppermute | solution.py:422
  41.7 15.6 %middle_group.1.inner2 = f32[4,22,48,128]{3,2,1,0:T(8,128)} custom-call(f32[4,64,64,128]{3,2,1,0:T(8,128)} %y.5, f32[64,64,128]{2,1,0:T(8,128)} %k.5, f32[64,64,128]{2,1,0:T(8,128)} %p.5, s32[16,8]{1,0:T(8,128)} %copy.10.count, s32[1,1,32]{2,1,0:T(1,128)} %order.5), custom_call_target="tpu_custom_call" | custom-call | flops 70778880 | bytes 5242880 | tf_op jit(solution)/shard_map/middle_group/pallas_call | solution.py:427
  57.3 0.0 collective-permute-done.2.h_east
  57.3 0.0 copy-start.2
  57.3 0.0 collective-permute-done.h_north
  57.3 0.0 copy-start.3
  57.3 0.0 collective-permute-done.1.h_south
  57.3 0.0 copy-start
  57.4 0.0 collective-permute-done.3.h_west
  57.4 0.0 copy-start.1
  57.4 0.6 copy-done.2
  58.0 0.1 copy-done.3
  58.0 0.1 copy-done
  58.1 0.1 copy-done.1
  58.2 23.3 %last_group.1 = f32[4,64,64,128]{3,2,1,0:T(8,128)} custom-call(f32[4,64,64,128]{3,2,1,0:T(8,128)} %y.5, f32[64,64,128]{2,1,0:T(8,128)} %k.5, f32[64,64,128]{2,1,0:T(8,128)} %p.5, f32[64,64,128]{2,1,0:T(8,128)} %u.3, f32[64,64,128]{2,1,0:T(8,128)} %v.3, s32[16,8]{1,0:T(8,128)} %copy.10.count, s32[1,1,32]{2,1,0:T(1,128)} %order.5, ...), custom_call_target="tpu_custom_call" | custom-call | flops 70778880 | bytes 5242880 | tf_op jit(solution)/shard_map/last_group/pallas_call | solution.py:438
Async XLA Ops:
  29.3 28.0 %collective-permute-start.1 = (f32[5,64,128]{2,1,0:T(8,128)}, f32[5,64,128]{2,1,0:T(8,128)S(1)}, u32[]{:S(2)}, u32[]{:S(2)}) collective-permute-start(f32[5,64,128]{2,1,0:T(8,128)} %get-tuple-element.14), channel_id=1, source_target_pairs={{0,1},{1,2},{2,3},{3,4},{4,5},{5,6},{6,7},{8,9},{9,10},{10,11},{11... | collective-permute-start | bytes 491528 | tf_op jit(solution)/shard_map/ppermute | solution.py:423
  32.8 24.6 %collective-permute-start.3 = (f32[5,64,128]{2,1,0:T(8,128)}, f32[5,64,128]{2,1,0:T(8,128)S(1)}, u32[]{:S(2)}, u32[]{:S(2)}) collective-permute-start(f32[5,64,128]{2,1,0:T(8,128)} %get-tuple-element.16), channel_id=1, source_target_pairs={{0,8},{8,16},{16,24},{24,32},{32,40},{40,48},{48,56},{56,64},{64,7... | collective-permute-start | bytes 491528 | tf_op jit(solution)/shard_map/ppermute | solution.py:425
  32.9 24.4 %collective-permute-start.2 = (f32[4,64,128]{2,1,0:T(8,128)}, f32[4,64,128]{2,1,0:T(8,128)S(1)}, u32[]{:S(2)}, u32[]{:S(2)}) collective-permute-start(f32[4,64,128]{2,1,0:T(8,128)} %get-tuple-element.15), channel_id=1, source_target_pairs={{8,0},{16,8},{24,16},{32,24},{40,32},{48,40},{56,48},{64,56},{72,6... | collective-permute-start | bytes 393224 | tf_op jit(solution)/shard_map/ppermute | solution.py:424
  38.5 18.8 %collective-permute-start = (f32[4,64,128]{2,1,0:T(8,128)}, f32[4,64,128]{2,1,0:T(8,128)S(1)}, u32[]{:S(2)}, u32[]{:S(2)}) collective-permute-start(f32[4,64,128]{2,1,0:T(8,128)} %get-tuple-element.13.own_row), channel_id=1, source_target_pairs={{1,0},{2,1},{3,2},{4,3},{5,4},{6,5},{7,6},{9,8},{10,9},{11,10},{12... | collective-permute-start | bytes 393224 | tf_op jit(solution)/shard_map/ppermute | solution.py:422
  57.3 0.7 copy-start.2
  57.3 0.7 copy-start.3
  57.3 0.8 copy-start
  57.4 0.8 copy-start.1

commit v2 on v0

v2 whole, which is shorter than its diff:
```python
import jax
import jax.numpy as jnp
import numpy as np
from jax import lax
from jax.experimental import pallas as pl
from jax.experimental.pallas import tpu as pltpu
from jax.sharding import PartitionSpec as P

SECTIONS = 12
LEV = 128
UNROLL = 32
TURNS = LEV // UNROLL
PAIRS = SECTIONS // 2 - 1
F32 = jnp.float32
ANY = pl.BlockSpec(memory_space=pl.ANY)
SMEM = pl.BlockSpec(memory_space=pltpu.SMEM)
MESH = pl.DeviceIdType.MESH


def section_table(sections):
    bvals = [1.0 / 3.0] * 3 + [
        (j * j + j - 2.0) / (2.0 * j * (j + 1.0)) for j in range(3, sections + 1)
    ]
    scale = 4.0 / (sections * sections + sections - 2.0)
    lead = [1.0, 1.0]
    for j in range(2, sections + 1):
        lead.append(lead[-1] * (2.0 * j - 1.0) / j)
    rows = []
    for j in range(1, sections + 1):
        keep, share = 1.0 - bvals[j - 1], bvals[j - 1]
        shift = keep / (share * lead[j - 1])
        product = scale * share * lead[j - 1] / 2.0
        back = (j - 1.0) / j * lead[j - 2] / lead[j] if j > 1 else 0.0
        rows.append((shift, product, scale * shift / 2.0, back))
    return scale, 1.0 - bvals[sections], bvals[sections] * lead[sections], rows


SCALE, KEEP, SHARE, TABLE = section_table(SECTIONS)


def level_rows(level):
    return pl.ds(pl.multiple_of(level * 8, 8), 8)


def sixth(n):
    return lax.shift_right_logical(n * 10923, 16)


def sweep(cur, columns, finish, titration_of, side):
    def step(i, carry):
        here, below = list(carry[:4]), list(carry[4:])
        side(i)
        for r in range(UNROLL):
            level = i * UNROLL + r
            rows, above_rows = level_rows(level), level_rows(level + 1)
            mixing = columns[4, rows, :]
            above = [cur[q, above_rows, :] for q in range(4)]
            upward = [mixing * (above[q] - here[q]) for q in range(4)]
            state = [(here[q] + upward[q]) - below[q] for q in range(4)]
            titration = titration_of(rows, here)
            split = columns[5, rows, :] * here[3]
            net = split - titration
            joined = (0.75 * SCALE) * here[1] - columns[6, rows, :] * here[0]
            finish(
                rows,
                here,
                [
                    state[0] + (joined - titration),
                    state[1] + (split - joined),
                    state[2] + net,
                    state[3] - net,
                ],
            )
            here, below = above, upward
        return (*here, *below)

    zero = jnp.zeros((8, LEV), F32)
    init = tuple(cur[q, pl.ds(0, 8), :] for q in range(4)) + (zero,) * 4
    lax.fori_loop(0, TURNS, step, init)


def store_all(ref, rows, values):
    for q in range(4):
        ref[q, rows, :] = values[q]


def day_steps(columns, work, lit, table, side, after_first=None, after_pairs=None, after_turn=None):
    ping, pong, tit, final = work
    columns[4, pl.ds(LEV * 8 - 8, 8), :] = jnp.zeros((8, LEV), F32)

    def first_titration(rows, here):
        product = here[0] * here[2]
        tit[rows, :] = product
        return (SCALE / 2.0) * product

    def first_finish(rows, here, state):
        store_all(ping, rows, state)
        store_all(pong, rows, here)

    sweep(columns, columns, first_finish, first_titration, lambda i: side(i, True))
    if after_first is not None:
        after_first()

    def titration_with(shift, product, offset):
        def titration(rows, here):
            ozone = here[0] + shift * columns[0, rows, :]
            nitric = here[2] + shift * columns[2, rows, :]
            return product * ozone * nitric - offset * tit[rows, :]

        return titration

    def middle(pair, half, cur, out):
        section = 1 + 2 * pair + half
        shift, product, offset, back = [table[section, c] for c in range(4)]

        def finish(rows, here, state):
            store_all(out, rows, [state[q] - back * out[q, rows, :] for q in range(4)])

        base = TURNS * (1 + 2 * pair + half)
        sweep(cur, columns, finish, titration_with(shift, product, offset), lambda i: side(base + i, False))

    def both(pair, carry):
        middle(pair, 0, ping, pong)
        middle(pair, 1, pong, ping)
        return carry

    lax.fori_loop(0, PAIRS, both, 0)
    if after_pairs is not None:
        after_pairs()
    shift, product, offset, back = TABLE[SECTIONS - 1]

    def last_finish(rows, here, state):
        start = [columns[q, rows, :] for q in range(4)]
        half = 0.5 * tit[rows, :]
        gain = 0.75 * start[1]
        night = [start[0] + (gain - half), start[1] - gain, start[2] - half, start[3] + half]
        for q in range(4):
            day = SHARE * (state[q] - back * pong[q, rows, :]) + KEEP * start[q]
            final[q, rows, :] = jnp.where(lit, day, night[q])

    base = TURNS * (SECTIONS - 1)
    sweep(ping, columns, last_finish, titration_with(shift, product, offset), lambda i: side(base + i, False))


def tile_in(nat, row0, columns, tile, plane):
    src = pl.ds(pl.multiple_of(row0 + tile * 128, 8), 128)
    dst = pl.ds(tile, 128, stride=8)
    factor = jnp.where(plane >= 4, SCALE, 1.0).astype(F32)
    turned = (factor * nat[plane, src, :]).T
    columns[plane, dst, :] = turned
    columns[6, dst, :] = 0.125 * turned


def tile_in_turn(nat, row0, columns, turn):
    tile = sixth(turn)
    tile_in(nat, row0, columns, tile, turn - 6 * tile)


def tile_in_all(nat, row0, columns, ready):
    turn = 0
    for tiles, wait in ready:
        wait()

        def step(tile, carry):
            for plane in range(6):
                tile_in(nat, row0, columns, tile, jnp.int32(plane))
            return carry

        lax.fori_loop(turn, turn + tiles, step, 0)
        turn += tiles


def tile_out(final, put, tile, q):
    put(tile, q, final[q, pl.ds(tile, 128, stride=8), :].T)


def tile_out_turn(final, put, turn, is_first):
    if is_first:
        tile_out(final, put, 0, turn)
    else:
        job = jnp.minimum(turn - TURNS, 27)
        tile_out(final, put, 1 + lax.shift_right_logical(job, 2), lax.bitwise_and(job, 3))


def lit_bits(count_ref, order_ref):
    count = count_ref[lax.axis_index("lat"), lax.axis_index("lon")]

    def mark(i, bits):
        bit = lax.shift_left(jnp.int32(1), order_ref[0, 0, i])
        return lax.bitwise_or(bits, jnp.where(i < count, bit, 0))

    return lax.fori_loop(0, 32, mark, jnp.int32(0))


def lit_columns(bits, longitude_of):
    tile = lax.broadcasted_iota(jnp.int32, (8, LEV), 0)
    lane = lax.broadcasted_iota(jnp.int32, (8, LEV), 1)
    octet = tile * 16 + lax.shift_right_logical(lane, 3)
    block = lax.shift_right_logical(longitude_of(octet), 1)
    return lax.bitwise_and(lax.shift_right_logical(jnp.full((8, LEV), bits, jnp.int32), block), 1) > 0


def inner_longitude(octet):
    place = sixth(octet)
    return jnp.where(place == 0, 0, jnp.where(place == 1, 63, place - 1))


class Copies:
    def __init__(self, sems):
        self.sems, self.used = sems, 0

    def start(self, pairs):
        group = []
        for src, dst in pairs:
            copy = pltpu.make_async_copy(src, dst, self.sems.at[self.used])
            self.used += 1
            copy.start()
            group.append(copy)
        return lambda: [copy.wait() for copy in group]


def flat(ref):
    return ref.reshape(*ref.shape[:-3], ref.shape[-3] * ref.shape[-2], LEV)


def planes(y, k, p, nat, lons, lats, to_lons, to_rows):
    return [
        (y.at[:, lons, lats], nat.at[pl.ds(0, 4), to_lons, to_rows]),
        (k.at[lons, lats], nat.at[4, to_lons, to_rows]),
        (p.at[lons, lats], nat.at[5, to_lons, to_rows]),
    ]


def clear_pads(*refs):
    for ref in refs:
        for q in range(4):
            ref[q, pl.ds(LEV * 8, 8), :] = jnp.zeros((8, LEV), F32)


ROWS48, ALL48 = pl.ds(8, 48), pl.ds(0, 48)


def edge_kernel(
    y, k, p, u, v, count, order, table,
    polar, inner1, turned, h_north, h_south, h_east, h_west,
    nat1, nat2, nat3, cols_a, cols_b, ping, pong, tit, final, to_south, to_north, to_west, to_east,
    send, recv, sems,
):
    lon, lat = lax.axis_index("lon"), lax.axis_index("lat")
    lons, lats = lax.axis_size("lon"), lax.axis_size("lat")
    west, east = lax.rem(lon + lons - 1, lons), lax.rem(lon + 1, lons)
    south, north = lax.rem(lat + lats - 1, lats), lax.rem(lat + 1, lats)
    barrier = pltpu.get_barrier_semaphore()
    for device in ({"lon": west}, {"lon": east}, {"lat": south}, {"lat": north}):
        pl.semaphore_signal(barrier, inc=1, device_id=device, device_id_type=MESH)

    copies = Copies(sems)
    ready = []
    for c in range(4):
        part = pl.ds(16 * c, 16)
        ready.append((2, copies.start(
            planes(y, k, p, nat1, part, pl.ds(0, 8), part, pl.ds(0, 8))
            + planes(y, k, p, nat1, part, pl.ds(56, 8), part, pl.ds(8, 8))
        )))
    second = copies.start(
        planes(y, k, p, nat2, pl.ds(0, 1), ROWS48, pl.ds(0, 1), ALL48)
        + planes(y, k, p, nat2, pl.ds(63, 1), ROWS48, pl.ds(1, 1), ALL48)
        + planes(y, k, p, nat2, pl.ds(1, 20), ROWS48, pl.ds(2, 20), ALL48)
    )
    third = copies.start(planes(y, k, p, nat3, pl.ds(20, 22), ROWS48, pl.ds(0, 22), ALL48))
    winds = copies.start([(u.at[63], to_east.at[4]), (v.at[:, 63], to_north.at[4])])
    bits = lit_bits(count, order)
    clear_pads(cols_a, cols_b, ping, pong)
    flat1, flat2, flat3 = flat(nat1), flat(nat2), flat(nat3)

    def put_in(nat):
        def put(tile, q, value):
            nat[q, pl.ds(pl.multiple_of(tile * 128, 8), 128), :] = value

        return put

    work = (ping, pong, tit, final)
    tile_in_all(flat1, 0, cols_a, ready)
    second()

    def side1(turn, is_first):
        tile_in_turn(flat2, 0, cols_b, turn)

    day_steps(cols_a, work, lit_columns(bits, lambda octet: lax.shift_right_logical(octet, 1)), table, side1)
    third()

    def side2(turn, is_first):
        tile_in_turn(flat3, 16, cols_a, turn)
        tile_out_turn(final, put_in(flat1), turn, is_first)

    staged = []

    def after_pairs2():
        staged.append(copies.start([
            (nat1.at[pl.ds(0, 4)], polar),
            (nat1.at[pl.ds(0, 4), :, 0], to_south),
            (nat1.at[pl.ds(0, 4), :, 15], to_north.at[pl.ds(0, 4)]),
            (nat1.at[pl.ds(0, 4), 0, pl.ds(0, 8)], to_west.at[:, pl.ds(0, 8)]),
            (nat1.at[pl.ds(0, 4), 0, pl.ds(8, 8)], to_west.at[:, pl.ds(56, 8)]),
            (nat1.at[pl.ds(0, 4), 63, pl.ds(0, 8)], to_east.at[pl.ds(0, 4), pl.ds(0, 8)]),
            (nat1.at[pl.ds(0, 4), 63, pl.ds(8, 8)], to_east.at[pl.ds(0, 4), pl.ds(56, 8)]),
        ]))

    def side2_last(turn, is_first):
        tile_in_turn(flat3, 16, cols_a, turn)

    def side2_all(turn, is_first):
        side2(turn, is_first) if (is_first or not staged) else side2_last(turn, is_first)

    day_steps(
        cols_b, work, lit_columns(bits, inner_longitude), table, side2_all, after_pairs=after_pairs2
    )
    staged[0]()
    winds()
    pl.semaphore_wait(barrier, 4)
    sends = []

    def send_to(index, src, dst, device):
        copy = pltpu.make_async_remote_copy(
            src_ref=src, dst_ref=dst, send_sem=send.at[index], recv_sem=recv.at[index],
            device_id=device, device_id_type=MESH,
        )
        copy.start()
        sends.append(copy)

    send_to(0, to_south, h_north, {"lat": south})
    send_to(1, to_north, h_south, {"lat": north})

    stored = []

    def side3(turn, is_first):
        if is_first or not stored:
            tile_out_turn(final, put_in(flat2), turn, is_first)

    def after_first3():
        copies.start([
            (nat2.at[pl.ds(0, 4), 0], to_west.at[:, pl.ds(8, 48)]),
            (nat2.at[pl.ds(0, 4), 1], to_east.at[pl.ds(0, 4), pl.ds(8, 48)]),
        ])()
        send_to(2, to_west, h_east, {"lon": west})
        send_to(3, to_east, h_west, {"lon": east})

    def after_pairs3():
        stored.append(copies.start([(nat2.at[pl.ds(0, 4)], inner1)]))

    day_steps(
        cols_a, work, lit_columns(bits, lambda octet: inner_longitude(octet + 128)), table, side3,
        after_first=after_first3, after_pairs=after_pairs3,
    )
    out = copies.start([(final, turned)])
    stored[0]()
    for copy in sends:
        copy.wait()
    out()


CHUNK = 4


def last_kernel(
    y, k, p, u, v, count, order, table, polar, inner1, turned, h_north, h_south, h_east, h_west,
    out,
    nat, cols, ping, pong, tit, final, before,
    mixed, uwind, vwind, first_row, s_halo, w_halo, south, eastward, northward, stage_out,
    out_sems, sems,
):
    copies = Copies(sems)
    ready = []
    for lon, span in ((0, 12), (12, 10)):
        part = pl.ds(lon, span)
        ready.append((4, copies.start(planes(y, k, p, nat, pl.ds(41 + lon, span), ROWS48, part, ALL48))))
    earlier = copies.start([(turned, before)])
    body = pl.ds(1, 64)
    lats = pl.ds(16, 48)
    filled = copies.start([
        (u, uwind),
        (v, vwind),
        (polar.at[:, :, 0], first_row),
        (h_south, s_halo),
        (h_west, w_halo),
        (h_north, mixed.at[:, body, 72]),
        (h_east, mixed.at[:, 65, pl.ds(8, 64)]),
        (polar.at[:, :, pl.ds(0, 8)], mixed.at[:, body, pl.ds(8, 8)]),
        (polar.at[:, :, pl.ds(8, 8)], mixed.at[:, body, pl.ds(64, 8)]),
        (inner1.at[:, 0], mixed.at[:, 1, lats]),
        (inner1.at[:, 1], mixed.at[:, 64, lats]),
        (inner1.at[:, pl.ds(2, 19)], mixed.at[:, pl.ds(2, 19), lats]),
        (inner1.at[:, 21, pl.ds(0, 16)], mixed.at[:, 21, pl.ds(16, 16)]),
    ])
    bits = lit_bits(count, order)
    clear_pads(cols, ping, pong)

    def put_from(octet0):
        def put(tile, q, value):
            for r in range(16):
                octet = octet0 + tile * 16 + r
                place = sixth(octet)
                dst = pl.ds(pl.multiple_of((octet - 6 * place) * 8 + 16, 8), 8)
                mixed[q, place, dst, :] = value[r * 8 : r * 8 + 8]

        return put

    tile_in_all(flat(nat), 32, cols, ready)
    earlier()

    def side(turn, is_first):
        tile_out_turn(before, put_from(128), turn, is_first)

    day_steps(
        cols, (ping, pong, tit, final),
        lit_columns(bits, lambda octet: sixth(octet + 256) - 1), table, side,
    )

    def finish_tile(tile, carry):
        for q in range(4):
            tile_out(final, put_from(256), tile, q)
        return carry

    lax.fori_loop(0, 8, finish_tile, 0)
    filled()

    @pl.when(lax.axis_index("lat") == lax.axis_size("lat") - 1)
    def _():
        def clear(i, carry):
            for q in range(4):
                mixed[q, i + 1, pl.ds(72, 1), :] = jnp.zeros((1, LEV), F32)
            return carry

        lax.fori_loop(0, 64, clear, 0)

    inside = jnp.where(lax.axis_index("lat") > 0, 1.0, 0.0).astype(F32)
    for m in range(8):
        rows = pl.ds(8 * m, 8)
        wind, gust = w_halo[4, rows, :], inside * s_halo[4, rows, :]
        for q in range(4):
            eastward[q, rows, :] = wind * jnp.where(
                wind > 0, w_halo[q, rows, :], mixed[q, 1, pl.ds(8 + 8 * m, 8), :]
            )
            south[q, rows, :] = gust * jnp.where(gust > 0, s_halo[q, rows, :], first_row[q, rows, :])

    def out_copy(chunk, slot):
        return pltpu.make_async_copy(
            stage_out.at[slot], out.at[:, pl.ds(chunk * CHUNK, CHUNK)], out_sems.at[slot]
        )

    def chunk_step(chunk, carry):
        slot = lax.rem(chunk, 2)

        @pl.when(chunk >= 2)
        def _():
            out_copy(chunk - 2, slot).wait()

        def lon_step(couple, inner_carry):
            for side_lon in range(2):
                lon = chunk * CHUNK + couple * 2 + side_lon
                for q in range(4):
                    northward[side_lon, q, pl.ds(7, 1), :] = south[q, pl.ds(lon, 1), :]
            lon = chunk * CHUNK + couple * 2
            for m in range(8):
                rows = pl.ds(8 * m, 8)
                here_rows, ahead_rows = pl.ds(8 + 8 * m, 8), pl.ds(9 + 8 * m, 8)
                west = [eastward[q, rows, :] for q in range(4)]
                here = [mixed[q, lon + 1, here_rows, :] for q in range(4)]
                for side_lon in range(2):
                    at = lon + side_lon
                    wind, gust = uwind[at, rows, :], vwind[at, rows, :]
                    wind_up, gust_up = wind > 0, gust > 0
                    for q in range(4):
                        beyond = mixed[q, at + 2, here_rows, :]
                        east = wind * jnp.where(wind_up, here[q], beyond)
                        north = gust * jnp.where(gust_up, here[q], mixed[q, at + 1, ahead_rows, :])
                        northward[side_lon, q, here_rows, :] = north
                        below = northward[side_lon, q, pl.ds(7 + 8 * m, 8), :]
                        stage_out[slot, q, couple * 2 + side_lon, rows, :] = (
                            here[q] - (east - west[q]) - (north - below)
                        )
                        west[q], here[q] = east, beyond
                for q in range(4):
                    eastward[q, rows, :] = west[q]
            return inner_carry

        lax.fori_loop(0, CHUNK // 2, lon_step, 0)
        out_copy(chunk, slot).start()
        return carry

    chunks = 64 // CHUNK
    lax.fori_loop(0, chunks, chunk_step, 0)
    for chunk in (chunks - 2, chunks - 1):
        out_copy(chunk, chunk % 2).wait()


def shape(*dims):
    return jax.ShapeDtypeStruct(dims, F32)


def vmem(*dims):
    return pltpu.VMEM(dims, F32)


COLUMNS = vmem(7, LEV * 8 + 8, LEV)
WORK = [
    vmem(4, LEV * 8 + 8, LEV),
    vmem(4, LEV * 8 + 8, LEV),
    vmem(LEV * 8, LEV),
    vmem(4, LEV * 8, LEV),
]
DMA = pltpu.SemaphoreType.DMA


def cost(groups):
    return pl.CostEstimate(
        flops=groups * 128 * 1024 * 540, bytes_accessed=groups * 5 * 2**20, transcendentals=0
    )


def body(tracers, kdiff, photolysis, u_wind, v_wind, day_count, day_order):
    inputs = (
        tracers, kdiff, photolysis, u_wind, v_wind, day_count.T, day_order,
        jnp.asarray(np.array(TABLE, np.float32)),
    )
    halos = (shape(4, 64, LEV), shape(5, 64, LEV), shape(4, 64, LEV), shape(5, 64, LEV))
    parts = pl.pallas_call(
        edge_kernel,
        name="edge_groups",
        out_shape=(shape(4, 64, 16, LEV), shape(4, 22, 48, LEV), shape(4, LEV * 8, LEV), *halos),
        in_specs=[ANY] * 5 + [SMEM] * 3,
        out_specs=(ANY,) * 7,
        scratch_shapes=[
            vmem(6, 64, 16, LEV), vmem(6, 22, 48, LEV), vmem(6, 22, 48, LEV),
            COLUMNS, COLUMNS, *WORK,
            vmem(4, 64, LEV), vmem(5, 64, LEV), vmem(4, 64, LEV), vmem(5, 64, LEV),
            DMA((4,)), DMA((4,)), DMA((64,)),
        ],
        compiler_params=pltpu.CompilerParams(
            vmem_limit_bytes=60 * 2**20, collective_id=0, has_side_effects=True
        ),
        cost_estimate=cost(3),
    )(*inputs)

    return pl.pallas_call(
        last_kernel,
        name="last_group",
        out_shape=shape(4, 64, 64, LEV),
        in_specs=[ANY] * 5 + [SMEM] * 3 + [ANY] * 7,
        out_specs=ANY,
        scratch_shapes=[
            vmem(6, 22, 48, LEV), COLUMNS, *WORK, vmem(4, LEV * 8, LEV),
            vmem(4, 66, 80, LEV),
            vmem(64, 64, LEV),
            vmem(64, 64, LEV),
            vmem(4, 64, LEV),
            vmem(5, 64, LEV),
            vmem(5, 64, LEV),
            vmem(4, 64, LEV),
            vmem(4, 64, LEV),
            vmem(2, 4, 72, LEV),
            vmem(2, 4, CHUNK, 64, LEV),
            DMA((2,)), DMA((24,)),
        ],
        compiler_params=pltpu.CompilerParams(vmem_limit_bytes=60 * 2**20),
        cost_estimate=cost(1),
    )(*inputs, *parts)


def solution(mesh):
    return jax.shard_map(
        body,
        mesh=mesh,
        in_specs=(
            P(None, "lon", "lat", None),
            P("lon", "lat", None),
            P("lon", "lat", None),
            P("lon", "lat", None),
            P("lon", "lat", None),
            P(),
            P("lon", "lat", None),
        ),
        out_specs=P(None, "lon", "lat", None),
        check_vma=False,
    )
```

time: 666 us -> 75.6 us (0.11)
  the two profiles are of different devices: /device:TPU:84 before, /device:TPU:2 now
where the time goes in v2:
time: 75.6 us; the launch traced here: 75.3 us
  Pallas kernels  75.3 us (100%)
    pallas_call x1, Pallas kernels, body(): pl.pallas_call(edge_kernel, name='edge_groups', out_shape=(shape(4, 64, 1...  48.6 us
    pallas_call x1, Pallas kernels, body(): pl.pallas_call(last_kernel, name='last_group', out_shape=shape(4, 64, 64,...  26.7 us

profile of v2, /device:TPU:2, one launch (start us, length us, event | category | flops | bytes accessed | tf_op | source)
XLA Modules:
  0.0 75.3 jit_solution(3088800376606313874)
XLA Ops:
  0.0 48.6 %edge_groups.1 = (f32[4,64,16,128]{3,2,1,0:T(8,128)}, f32[4,22,48,128]{3,2,1,0:T(8,128)}, f32[4,1024,128]{2,1,0:T(8,128)}, f32[4,64,128]{2,1,0:T(8,128)}, f32[5,...) custom-call(f32[4,64,64,128]{3,2,1,0:T(8,128)} %y.3, f32[64,64,128]{2,1,0:T(8,128)} %k.3, ...), custom_call_target="tpu_custom_call" | custom-call | flops 212336640 | bytes 15728640 | tf_op jit(solution)/shard_map/edge_groups/pallas_call | solution.py:527
  48.6 26.7 %last_group.1 = f32[4,64,64,128]{3,2,1,0:T(8,128)} custom-call(f32[4,64,64,128]{3,2,1,0:T(8,128)} %y.3, f32[64,64,128]{2,1,0:T(8,128)} %k.3, f32[64,64,128]{2,1,0:T(8,128)} %p.3, f32[64,64,128]{2,1,0:T(8,128)} %u.3, f32[64,64,128]{2,1,0:T(8,128)} %v.3, s32[8,16]{1,0:T(8,128)} %bitcast.2, s32[1,1,32]{2,1,0:T(1,128)} %order.3, f32[12,4]{1,0:T(8,128)} %constant.2.clone.table, ...), custom_call_target="tpu_custom_call" | custom-call | flops 70778880 | bytes 5242880 | tf_op jit(solution)/shard_map/last_group/pallas_call | solution.py:545

commit v3 on v2

--- a/solution.py
+++ b/solution.py
@@ -46,11 +46,12 @@
     return lax.shift_right_logical(n * 10923, 16)
 
 
-def sweep(cur, columns, finish, titration_of, side):
+def sweep(cur, columns, finish, titration_of, side, turn_end=None):
     def step(i, carry):
         here, below = list(carry[:4]), list(carry[4:])
-        side(i)
         for r in range(UNROLL):
+            if r == 8:
+                side(i)
             level = i * UNROLL + r
             rows, above_rows = level_rows(level), level_rows(level + 1)
             mixing = columns[4, rows, :]
@@ -72,6 +73,8 @@
                 ],
             )
             here, below = above, upward
+        if turn_end is not None:
+            turn_end(i)
         return (*here, *below)
 
     zero = jnp.zeros((8, LEV), F32)
@@ -84,7 +87,7 @@
         ref[q, rows, :] = values[q]
 
 
-def day_steps(columns, work, lit, table, side, after_first=None, after_pairs=None, after_turn=None):
+def day_steps(columns, work, lit, table, side, after_first=None, after_pairs=None, turn_end=None):
     ping, pong, tit, final = work
     columns[4, pl.ds(LEV * 8 - 8, 8), :] = jnp.zeros((8, LEV), F32)
 
@@ -97,7 +100,7 @@
         store_all(ping, rows, state)
         store_all(pong, rows, here)
 
-    sweep(columns, columns, first_finish, first_titration, lambda i: side(i, True))
+    sweep(columns, columns, first_finish, first_titration, lambda i: side(i, "first"))
     if after_first is not None:
         after_first()
 
@@ -117,7 +120,7 @@
             store_all(out, rows, [state[q] - back * out[q, rows, :] for q in range(4)])
 
         base = TURNS * (1 + 2 * pair + half)
-        sweep(cur, columns, finish, titration_with(shift, product, offset), lambda i: side(base + i, False))
+        sweep(cur, columns, finish, titration_with(shift, product, offset), lambda i: side(base + i, "middle"))
 
     def both(pair, carry):
         middle(pair, 0, ping, pong)
@@ -139,45 +142,52 @@
             final[q, rows, :] = jnp.where(lit, day, night[q])
 
     base = TURNS * (SECTIONS - 1)
-    sweep(ping, columns, last_finish, titration_with(shift, product, offset), lambda i: side(base + i, False))
+    sweep(ping, columns, last_finish, titration_with(shift, product, offset), lambda i: side(base + i, "last"), turn_end)
 
 
 def tile_in(nat, row0, columns, tile, plane):
     src = pl.ds(pl.multiple_of(row0 + tile * 128, 8), 128)
     dst = pl.ds(tile, 128, stride=8)
-    factor = jnp.where(plane >= 4, SCALE, 1.0).astype(F32)
-    turned = (factor * nat[plane, src, :]).T
+    turned = nat[plane, src, :].T
+    if isinstance(plane, int) and plane >= 4:
+        turned = SCALE * turned
     columns[plane, dst, :] = turned
-    columns[6, dst, :] = 0.125 * turned
-
-
-def tile_in_turn(nat, row0, columns, turn):
-    tile = sixth(turn)
-    tile_in(nat, row0, columns, tile, turn - 6 * tile)
+    if isinstance(plane, int) and plane == 5:
+        columns[6, dst, :] = 0.125 * turned
+
+
+def tile_in_turn(nat, row0, columns, turn, stage):
+    if stage == "middle":
+        job = jnp.minimum(turn - TURNS, 31)
+        tile_in(nat, row0, columns, lax.shift_right_logical(job, 2), lax.bitwise_and(job, 3))
+    else:
+        plane, turn0 = (4, 0) if stage == "first" else (5, TURNS * (SECTIONS - 1))
+        for half in range(2):
+            tile_in(nat, row0, columns, 2 * (turn - turn0) + half, plane)
 
 
 def tile_in_all(nat, row0, columns, ready):
-    turn = 0
+    done = 0
     for tiles, wait in ready:
         wait()
 
         def step(tile, carry):
             for plane in range(6):
-                tile_in(nat, row0, columns, tile, jnp.int32(plane))
+                tile_in(nat, row0, columns, tile, plane)
             return carry
 
-        lax.fori_loop(turn, turn + tiles, step, 0)
-        turn += tiles
+        lax.fori_loop(done, done + tiles, step, 0)
+        done += tiles
 
 
 def tile_out(final, put, tile, q):
     put(tile, q, final[q, pl.ds(tile, 128, stride=8), :].T)
 
 
-def tile_out_turn(final, put, turn, is_first):
-    if is_first:
+def tile_out_turn(final, put, turn, stage):
+    if stage == "first":
         tile_out(final, put, 0, turn)
-    else:
+    elif stage == "middle":
         job = jnp.minimum(turn - TURNS, 27)
         tile_out(final, put, 1 + lax.shift_right_logical(job, 2), lax.bitwise_and(job, 3))
 
@@ -240,11 +250,11 @@
 ROWS48, ALL48 = pl.ds(8, 48), pl.ds(0, 48)
 
 
-def edge_kernel(
+def day_kernel(
     y, k, p, u, v, count, order, table,
-    polar, inner1, turned, h_north, h_south, h_east, h_west,
-    nat1, nat2, nat3, cols_a, cols_b, ping, pong, tit, final, to_south, to_north, to_west, to_east,
-    send, recv, sems,
+    polar, inner1, inner2, turned, h_north, h_south, h_east, h_west,
+    nat1, nat2, nat3, nat4, cols_a, cols_b, ping, pong, tit, final, to_south, to_north, to_west, to_east,
+    send, recv, turn_sems, sems,
 ):
     lon, lat = lax.axis_index("lon"), lax.axis_index("lat")
     lons, lats = lax.axis_size("lon"), lax.axis_size("lat")
@@ -262,36 +272,42 @@
             planes(y, k, p, nat1, part, pl.ds(0, 8), part, pl.ds(0, 8))
             + planes(y, k, p, nat1, part, pl.ds(56, 8), part, pl.ds(8, 8))
         )))
-    second = copies.start(
-        planes(y, k, p, nat2, pl.ds(0, 1), ROWS48, pl.ds(0, 1), ALL48)
-        + planes(y, k, p, nat2, pl.ds(63, 1), ROWS48, pl.ds(1, 1), ALL48)
-        + planes(y, k, p, nat2, pl.ds(1, 20), ROWS48, pl.ds(2, 20), ALL48)
-    )
-    third = copies.start(planes(y, k, p, nat3, pl.ds(20, 22), ROWS48, pl.ds(0, 22), ALL48))
-    winds = copies.start([(u.at[63], to_east.at[4]), (v.at[:, 63], to_north.at[4])])
     bits = lit_bits(count, order)
     clear_pads(cols_a, cols_b, ping, pong)
-    flat1, flat2, flat3 = flat(nat1), flat(nat2), flat(nat3)
-
-    def put_in(nat):
+    flat1, flat2, flat3, flat4 = flat(nat1), flat(nat2), flat(nat3), flat(nat4)
+
+    def put_in(nat, row0=0):
         def put(tile, q, value):
-            nat[q, pl.ds(pl.multiple_of(tile * 128, 8), 128), :] = value
+            nat[q, pl.ds(pl.multiple_of(row0 + tile * 128, 8), 128), :] = value
 
         return put
 
     work = (ping, pong, tit, final)
-    tile_in_all(flat1, 0, cols_a, ready)
-    second()
-
-    def side1(turn, is_first):
-        tile_in_turn(flat2, 0, cols_b, turn)
+    later = []
+
+    def second_part():
+        ready[1][1]()
+        later.append(copies.start(
+            planes(y, k, p, nat2, pl.ds(0, 1), ROWS48, pl.ds(0, 1), ALL48)
+            + planes(y, k, p, nat2, pl.ds(63, 1), ROWS48, pl.ds(1, 1), ALL48)
+            + planes(y, k, p, nat2, pl.ds(1, 20), ROWS48, pl.ds(2, 20), ALL48)
+        ))
+
+    tile_in_all(flat1, 0, cols_a, [ready[0], (2, second_part), *ready[2:]])
+    later[0]()
+    third = copies.start(planes(y, k, p, nat3, pl.ds(20, 22), ROWS48, pl.ds(0, 22), ALL48))
+    fourth = copies.start(planes(y, k, p, nat4, pl.ds(41, 22), ROWS48, pl.ds(0, 22), ALL48))
+    winds = copies.start([(u.at[63], to_east.at[4]), (v.at[:, 63], to_north.at[4])])
+
+    def side1(turn, stage):
+        tile_in_turn(flat2, 0, cols_b, turn, stage)
 
     day_steps(cols_a, work, lit_columns(bits, lambda octet: lax.shift_right_logical(octet, 1)), table, side1)
     third()
 
-    def side2(turn, is_first):
-        tile_in_turn(flat3, 16, cols_a, turn)
-        tile_out_turn(final, put_in(flat1), turn, is_first)
+    def side2(turn, stage):
+        tile_in_turn(flat3, 16, cols_a, turn, stage)
+        tile_out_turn(final, put_in(flat1), turn, stage)
 
     staged = []
 
@@ -306,14 +322,8 @@
             (nat1.at[pl.ds(0, 4), 63, pl.ds(8, 8)], to_east.at[pl.ds(0, 4), pl.ds(56, 8)]),
         ]))
 
-    def side2_last(turn, is_first):
-        tile_in_turn(flat3, 16, cols_a, turn)
-
-    def side2_all(turn, is_first):
-        side2(turn, is_first) if (is_first or not staged) else side2_last(turn, is_first)
-
     day_steps(
-        cols_b, work, lit_columns(bits, inner_longitude), table, side2_all, after_pairs=after_pairs2
+        cols_b, work, lit_columns(bits, inner_longitude), table, side2, after_pairs=after_pairs2
     )
     staged[0]()
     winds()
@@ -333,9 +343,11 @@
 
     stored = []
 
-    def side3(turn, is_first):
-        if is_first or not stored:
-            tile_out_turn(final, put_in(flat2), turn, is_first)
+    fourth()
+
+    def side3(turn, stage):
+        tile_in_turn(flat4, 32, cols_b, turn, stage)
+        tile_out_turn(final, put_in(flat2), turn, stage)
 
     def after_first3():
         copies.start([
@@ -345,6 +357,10 @@
         send_to(2, to_west, h_east, {"lon": west})
         send_to(3, to_east, h_west, {"lon": east})
 
+    def turned_part(i):
+        rows = pl.ds(pl.multiple_of(i * UNROLL * 8, 8), UNROLL * 8)
+        return pltpu.make_async_copy(final.at[:, rows], turned.at[:, rows], turn_sems.at[i])
+
     def after_pairs3():
         stored.append(copies.start([(nat2.at[pl.ds(0, 4)], inner1)]))
 
@@ -352,34 +368,39 @@
         cols_a, work, lit_columns(bits, lambda octet: inner_longitude(octet + 128)), table, side3,
         after_first=after_first3, after_pairs=after_pairs3,
     )
-    out = copies.start([(final, turned)])
+
+    def side4(turn, stage):
+        tile_out_turn(final, put_in(flat3, 16), turn, stage)
+
+    def after_pairs4():
+        stored.append(copies.start([(nat3.at[pl.ds(0, 4)], inner2)]))
+
+    day_steps(
+        cols_b, work, lit_columns(bits, lambda octet: sixth(octet + 256) - 1), table, side4,
+        after_pairs=after_pairs4, turn_end=lambda i: turned_part(i).start(),
+    )
     stored[0]()
+    stored[1]()
     for copy in sends:
         copy.wait()
-    out()
+    for i in range(TURNS):
+        turned_part(i).wait()
 
 
 CHUNK = 4
 
 
-def last_kernel(
-    y, k, p, u, v, count, order, table, polar, inner1, turned, h_north, h_south, h_east, h_west,
+def transport_kernel(
+    u, v, polar, inner1, inner2, turned, h_north, h_south, h_east, h_west,
     out,
-    nat, cols, ping, pong, tit, final, before,
-    mixed, uwind, vwind, first_row, s_halo, w_halo, south, eastward, northward, stage_out,
+    before, mixed, uwind, vwind, first_row, s_halo, w_halo, south, eastward, northward, stage_out,
     out_sems, sems,
 ):
     copies = Copies(sems)
-    ready = []
-    for lon, span in ((0, 12), (12, 10)):
-        part = pl.ds(lon, span)
-        ready.append((4, copies.start(planes(y, k, p, nat, pl.ds(41 + lon, span), ROWS48, part, ALL48))))
-    earlier = copies.start([(turned, before)])
     body = pl.ds(1, 64)
     lats = pl.ds(16, 48)
+    earlier = copies.start([(turned, before)])
     filled = copies.start([
-        (u, uwind),
-        (v, vwind),
         (polar.at[:, :, 0], first_row),
         (h_south, s_halo),
         (h_west, w_halo),
@@ -391,34 +412,25 @@
         (inner1.at[:, 1], mixed.at[:, 64, lats]),
         (inner1.at[:, pl.ds(2, 19)], mixed.at[:, pl.ds(2, 19), lats]),
         (inner1.at[:, 21, pl.ds(0, 16)], mixed.at[:, 21, pl.ds(16, 16)]),
+        (inner2.at[:, 0, pl.ds(16, 32)], mixed.at[:, 21, pl.ds(32, 32)]),
+        (inner2.at[:, pl.ds(1, 20)], mixed.at[:, pl.ds(22, 20), lats]),
+        (inner2.at[:, 21, pl.ds(0, 32)], mixed.at[:, 42, pl.ds(16, 32)]),
+        (u, uwind),
+        (v, vwind),
     ])
-    bits = lit_bits(count, order)
-    clear_pads(cols, ping, pong)
-
-    def put_from(octet0):
-        def put(tile, q, value):
-            for r in range(16):
-                octet = octet0 + tile * 16 + r
-                place = sixth(octet)
-                dst = pl.ds(pl.multiple_of((octet - 6 * place) * 8 + 16, 8), 8)
-                mixed[q, place, dst, :] = value[r * 8 : r * 8 + 8]
-
-        return put
-
-    tile_in_all(flat(nat), 32, cols, ready)
+
+    def put(tile, q, value):
+        for r in range(16):
+            octet = 256 + tile * 16 + r
+            place = sixth(octet)
+            dst = pl.ds(pl.multiple_of((octet - 6 * place) * 8 + 16, 8), 8)
+            mixed[q, place, dst, :] = value[r * 8 : r * 8 + 8]
+
     earlier()
-
-    def side(turn, is_first):
-        tile_out_turn(before, put_from(128), turn, is_first)
-
-    day_steps(
-        cols, (ping, pong, tit, final),
-        lit_columns(bits, lambda octet: sixth(octet + 256) - 1), table, side,
-    )
 
     def finish_tile(tile, carry):
         for q in range(4):
-            tile_out(final, put_from(256), tile, q)
+            tile_out(before, put, tile, q)
         return carry
 
     lax.fori_loop(0, 8, finish_tile, 0)
@@ -443,18 +455,12 @@
             )
             south[q, rows, :] = gust * jnp.where(gust > 0, s_halo[q, rows, :], first_row[q, rows, :])
 
-    def out_copy(chunk, slot):
+    def out_copy(chunk):
         return pltpu.make_async_copy(
-            stage_out.at[slot], out.at[:, pl.ds(chunk * CHUNK, CHUNK)], out_sems.at[slot]
+            stage_out.at[chunk], out.at[:, pl.ds(chunk * CHUNK, CHUNK)], out_sems.at[chunk]
         )
 
     def chunk_step(chunk, carry):
-        slot = lax.rem(chunk, 2)
-
-        @pl.when(chunk >= 2)
-        def _():
-            out_copy(chunk - 2, slot).wait()
-
         def lon_step(couple, inner_carry):
             for side_lon in range(2):
                 lon = chunk * CHUNK + couple * 2 + side_lon
@@ -476,7 +482,7 @@
                         north = gust * jnp.where(gust_up, here[q], mixed[q, at + 1, ahead_rows, :])
                         northward[side_lon, q, here_rows, :] = north
                         below = northward[side_lon, q, pl.ds(7 + 8 * m, 8), :]
-                        stage_out[slot, q, couple * 2 + side_lon, rows, :] = (
+                        stage_out[chunk, q, couple * 2 + side_lon, rows, :] = (
                             here[q] - (east - west[q]) - (north - below)
                         )
                         west[q], here[q] = east, beyond
@@ -485,13 +491,16 @@
             return inner_carry
 
         lax.fori_loop(0, CHUNK // 2, lon_step, 0)
-        out_copy(chunk, slot).start()
+        out_copy(chunk).start()
         return carry
 
-    chunks = 64 // CHUNK
-    lax.fori_loop(0, chunks, chunk_step, 0)
-    for chunk in (chunks - 2, chunks - 1):
-        out_copy(chunk, chunk % 2).wait()
+    lax.fori_loop(0, 64 // CHUNK, chunk_step, 0)
+
+    def finish_chunk(chunk, carry):
+        out_copy(chunk).wait()
+        return carry
+
+    lax.fori_loop(0, 64 // CHUNK, finish_chunk, 0)
 
 
 def shape(*dims):
@@ -525,31 +534,34 @@
     )
     halos = (shape(4, 64, LEV), shape(5, 64, LEV), shape(4, 64, LEV), shape(5, 64, LEV))
     parts = pl.pallas_call(
-        edge_kernel,
-        name="edge_groups",
-        out_shape=(shape(4, 64, 16, LEV), shape(4, 22, 48, LEV), shape(4, LEV * 8, LEV), *halos),
+        day_kernel,
+        name="day_groups",
+        out_shape=(
+            shape(4, 64, 16, LEV), shape(4, 22, 48, LEV), shape(4, 22, 48, LEV), shape(4, LEV * 8, LEV),
+            *halos,
+        ),
         in_specs=[ANY] * 5 + [SMEM] * 3,
-        out_specs=(ANY,) * 7,
+        out_specs=(ANY,) * 8,
         scratch_shapes=[
-            vmem(6, 64, 16, LEV), vmem(6, 22, 48, LEV), vmem(6, 22, 48, LEV),
+            vmem(6, 64, 16, LEV), vmem(6, 22, 48, LEV), vmem(6, 22, 48, LEV), vmem(6, 22, 48, LEV),
             COLUMNS, COLUMNS, *WORK,
             vmem(4, 64, LEV), vmem(5, 64, LEV), vmem(4, 64, LEV), vmem(5, 64, LEV),
-            DMA((4,)), DMA((4,)), DMA((64,)),
+            DMA((4,)), DMA((4,)), DMA((TURNS,)), DMA((64,)),
         ],
         compiler_params=pltpu.CompilerParams(
             vmem_limit_bytes=60 * 2**20, collective_id=0, has_side_effects=True
         ),
-        cost_estimate=cost(3),
+        cost_estimate=cost(4),
     )(*inputs)
 
     return pl.pallas_call(
-        last_kernel,
-        name="last_group",
+        transport_kernel,
+        name="transport",
         out_shape=shape(4, 64, 64, LEV),
-        in_specs=[ANY] * 5 + [SMEM] * 3 + [ANY] * 7,
+        in_specs=[ANY] * 10,
         out_specs=ANY,
         scratch_shapes=[
-            vmem(6, 22, 48, LEV), COLUMNS, *WORK, vmem(4, LEV * 8, LEV),
+            vmem(4, LEV * 8, LEV),
             vmem(4, 66, 80, LEV),
             vmem(64, 64, LEV),
             vmem(64, 64, LEV),
@@ -559,12 +571,12 @@
             vmem(4, 64, LEV),
             vmem(4, 64, LEV),
             vmem(2, 4, 72, LEV),
-            vmem(2, 4, CHUNK, 64, LEV),
-            DMA((2,)), DMA((24,)),
+            vmem(64 // CHUNK, 4, CHUNK, 64, LEV),
+            DMA((64 // CHUNK,)), DMA((24,)),
         ],
         compiler_params=pltpu.CompilerParams(vmem_limit_bytes=60 * 2**20),
-        cost_estimate=cost(1),
-    )(*inputs, *parts)
+        cost_estimate=pl.CostEstimate(flops=2**21 * 10, bytes_accessed=20 * 2**20, transcendentals=0),
+    )(u_wind, v_wind, *parts)
 
 
 def solution(mesh):

time: 75.6 us -> 66.6 us (0.88)
  Pallas kernels: 75.3 us -> 66.1 us
    pallas_call x2, Pallas kernels: 75.3 us -> 66.1 us  [the longest x1 56.1 us: body(): pl.pallas_call(day_kernel, name='day_groups', out_shape=(shape(4, 64, 16,...]
where the time goes in v3:
time: 66.6 us; the launch traced here: 66.1 us
  Pallas kernels  66.1 us (99%)
    pallas_call x1, Pallas kernels, body(): pl.pallas_call(day_kernel, name='day_groups', out_shape=(shape(4, 64, 16,...  56.1 us
    pallas_call x1, Pallas kernels, body(): pl.pallas_call(transport_kernel, name='transport', out_shape=shape(4, 64,...  9.96 us

profile of v3, /device:TPU:2, one launch (start us, length us, event | category | flops | bytes accessed | tf_op | source)
XLA Modules:
  0.0 66.1 jit_solution(10379023462215687603)
XLA Ops:
  0.0 56.1 %day_groups.1 = (f32[4,64,16,128]{3,2,1,0:T(8,128)}, f32[4,22,48,128]{3,2,1,0:T(8,128)}, f32[4,22,48,128]{3,2,1,0:T(8,128)}, f32[4,1024,128]{2,1,0:T(8,128)}, f3...) custom-call(f32[4,64,64,128]{3,2,1,0:T(8,128)} %y.1, ...), custom_call_target="tpu_custom_call" | custom-call | flops 283115520 | bytes 20971520 | tf_op jit(solution)/shard_map/day_groups/pallas_call | solution.py:536
  56.1 10.0 %transport.1 = f32[4,64,64,128]{3,2,1,0:T(8,128)} custom-call(f32[64,64,128]{2,1,0:T(8,128)} %u.3, f32[64,64,128]{2,1,0:T(8,128)} %v.3, f32[4,64,16,128]{3,2,1,0:T(8,128)} %get-tuple-element.13.polar, f32[4,22,48,128]{3,2,1,0:T(8,128)} %get-tuple-element.14.inner1, f32[4,22,48,128]{3,2,1,0:T(8,128)} %get-tuple-element.15.inner2, ...), custom_call_target="tpu_custom_call" | custom-call | flops 20971520 | bytes 20971520 | tf_op jit(solution)/shard_map/transport/pallas_call | solution.py:557

commit v4 on v3

--- a/solution.py
+++ b/solution.py
@@ -112,7 +112,7 @@
 
         return titration
 
-    def middle(pair, half, cur, out):
+    def middle(pair, half, cur, out, busy=True):
         section = 1 + 2 * pair + half
         shift, product, offset, back = [table[section, c] for c in range(4)]
 
@@ -120,16 +120,18 @@
             store_all(out, rows, [state[q] - back * out[q, rows, :] for q in range(4)])
 
         base = TURNS * (1 + 2 * pair + half)
-        sweep(cur, columns, finish, titration_with(shift, product, offset), lambda i: side(base + i, "middle"))
+        sweep(cur, columns, finish, titration_with(shift, product, offset), lambda i: side(base + i, "middle") if busy else None)
 
     def both(pair, carry):
         middle(pair, 0, ping, pong)
         middle(pair, 1, pong, ping)
         return carry
 
-    lax.fori_loop(0, PAIRS, both, 0)
+    lax.fori_loop(0, PAIRS - 1, both, 0)
     if after_pairs is not None:
         after_pairs()
+    middle(PAIRS - 1, 0, ping, pong, False)
+    middle(PAIRS - 1, 1, pong, ping, False)
     shift, product, offset, back = TABLE[SECTIONS - 1]
 
     def last_finish(rows, here, state):
@@ -158,7 +160,7 @@
 
 def tile_in_turn(nat, row0, columns, turn, stage):
     if stage == "middle":
-        job = jnp.minimum(turn - TURNS, 31)
+        job = turn - TURNS
         tile_in(nat, row0, columns, lax.shift_right_logical(job, 2), lax.bitwise_and(job, 3))
     else:
         plane, turn0 = (4, 0) if stage == "first" else (5, TURNS * (SECTIONS - 1))
@@ -399,24 +401,42 @@
     copies = Copies(sems)
     body = pl.ds(1, 64)
     lats = pl.ds(16, 48)
-    earlier = copies.start([(turned, before)])
-    filled = copies.start([
+
+    def strips(lon, span):
+        src, dst = pl.ds(lon, span), pl.ds(lon + 1, span)
+        return [
+            (polar.at[:, src, pl.ds(0, 8)], mixed.at[:, dst, pl.ds(8, 8)]),
+            (polar.at[:, src, pl.ds(8, 8)], mixed.at[:, dst, pl.ds(64, 8)]),
+        ]
+
+    def winds(lon, span):
+        lons = pl.ds(lon, span)
+        return [(u.at[lons], uwind.at[lons]), (v.at[lons], vwind.at[lons])]
+
+    west_part = copies.start([
         (polar.at[:, :, 0], first_row),
         (h_south, s_halo),
         (h_west, w_halo),
         (h_north, mixed.at[:, body, 72]),
         (h_east, mixed.at[:, 65, pl.ds(8, 64)]),
-        (polar.at[:, :, pl.ds(0, 8)], mixed.at[:, body, pl.ds(8, 8)]),
-        (polar.at[:, :, pl.ds(8, 8)], mixed.at[:, body, pl.ds(64, 8)]),
+        *strips(0, 18),
         (inner1.at[:, 0], mixed.at[:, 1, lats]),
-        (inner1.at[:, 1], mixed.at[:, 64, lats]),
         (inner1.at[:, pl.ds(2, 19)], mixed.at[:, pl.ds(2, 19), lats]),
         (inner1.at[:, 21, pl.ds(0, 16)], mixed.at[:, 21, pl.ds(16, 16)]),
+        *winds(0, 16),
+    ])
+    middle_part = copies.start([
+        *strips(18, 24),
         (inner2.at[:, 0, pl.ds(16, 32)], mixed.at[:, 21, pl.ds(32, 32)]),
         (inner2.at[:, pl.ds(1, 20)], mixed.at[:, pl.ds(22, 20), lats]),
         (inner2.at[:, 21, pl.ds(0, 32)], mixed.at[:, 42, pl.ds(16, 32)]),
-        (u, uwind),
-        (v, vwind),
+        *winds(16, 24),
+    ])
+    east_part = copies.start([
+        (turned, before),
+        *strips(42, 22),
+        (inner1.at[:, 1], mixed.at[:, 64, lats]),
+        *winds(40, 24),
     ])
 
     def put(tile, q, value):
@@ -426,15 +446,12 @@
             dst = pl.ds(pl.multiple_of((octet - 6 * place) * 8 + 16, 8), 8)
             mixed[q, place, dst, :] = value[r * 8 : r * 8 + 8]
 
-    earlier()
-
     def finish_tile(tile, carry):
         for q in range(4):
             tile_out(before, put, tile, q)
         return carry
 
-    lax.fori_loop(0, 8, finish_tile, 0)
-    filled()
+    west_part()
 
     @pl.when(lax.axis_index("lat") == lax.axis_size("lat") - 1)
     def _():
@@ -494,7 +511,12 @@
         out_copy(chunk).start()
         return carry
 
-    lax.fori_loop(0, 64 // CHUNK, chunk_step, 0)
+    lax.fori_loop(0, 16 // CHUNK, chunk_step, 0)
+    middle_part()
+    lax.fori_loop(16 // CHUNK, 40 // CHUNK, chunk_step, 0)
+    east_part()
+    lax.fori_loop(0, 8, finish_tile, 0)
+    lax.fori_loop(40 // CHUNK, 64 // CHUNK, chunk_step, 0)
 
     def finish_chunk(chunk, carry):
         out_copy(chunk).wait()
@@ -572,7 +594,7 @@
             vmem(4, 64, LEV),
             vmem(2, 4, 72, LEV),
             vmem(64 // CHUNK, 4, CHUNK, 64, LEV),
-            DMA((64 // CHUNK,)), DMA((24,)),
+            DMA((64 // CHUNK,)), DMA((32,)),
         ],
         compiler_params=pltpu.CompilerParams(vmem_limit_bytes=60 * 2**20),
         cost_estimate=pl.CostEstimate(flops=2**21 * 10, bytes_accessed=20 * 2**20, transcendentals=0),

time: 66.6 us -> 65.2 us (0.979)
  Pallas kernels: 66.1 us -> 65 us
    pallas_call x1, Pallas kernels: 56.1 us -> 54.3 us  [body(): pl.pallas_call(day_kernel, name='day_groups', out_shape=(shape(4, 64, 16,...]
    pallas_call x1, Pallas kernels: 9.96 us -> 10.7 us  [body(): pl.pallas_call(transport_kernel, name='transport', out_shape=shape(4, 64,...]
where the time goes in v4:
time: 65.2 us; the launch traced here: 65 us
  Pallas kernels  65 us (100%)
    pallas_call x1, Pallas kernels, body(): pl.pallas_call(day_kernel, name='day_groups', out_shape=(shape(4, 64, 16,...  54.3 us
    pallas_call x1, Pallas kernels, body(): pl.pallas_call(transport_kernel, name='transport', out_shape=shape(4, 64,...  10.7 us

profile of v4, /device:TPU:2, one launch (start us, length us, event | category | flops | bytes accessed | tf_op | source)
XLA Modules:
  0.0 65.0 jit_solution(16064641024304416538)
XLA Ops:
  0.0 54.3 %day_groups.1 = (f32[4,64,16,128]{3,2,1,0:T(8,128)}, f32[4,22,48,128]{3,2,1,0:T(8,128)}, f32[4,22,48,128]{3,2,1,0:T(8,128)}, f32[4,1024,128]{2,1,0:T(8,128)}, f3...) custom-call(f32[4,64,64,128]{3,2,1,0:T(8,128)} %y.1, ...), custom_call_target="tpu_custom_call" | custom-call | flops 283115520 | bytes 20971520 | tf_op jit(solution)/shard_map/day_groups/pallas_call | solution.py:558
  54.3 10.7 %transport.1 = f32[4,64,64,128]{3,2,1,0:T(8,128)} custom-call(f32[64,64,128]{2,1,0:T(8,128)} %u.3, f32[64,64,128]{2,1,0:T(8,128)} %v.3, f32[4,64,16,128]{3,2,1,0:T(8,128)} %get-tuple-element.13.polar, f32[4,22,48,128]{3,2,1,0:T(8,128)} %get-tuple-element.14.inner1, f32[4,22,48,128]{3,2,1,0:T(8,128)} %get-tuple-element.15.inner2, ...), custom_call_target="tpu_custom_call" | custom-call | flops 20971520 | bytes 20971520 | tf_op jit(solution)/shard_map/transport/pallas_call | solution.py:579
